TPU v7x, 1024 devices: a whole 8x8x8 slice. The times are simulated.
1024 devices in a mesh: dp: 16 (over x, core), mp: 8 (over z), rep: 8 (over y).
Axes of the slice: x: 8, y: 8, z: 8, core: 2. Of those that a mesh axis runs over, the one named last changes fastest.
Arguments:
- query_rows: bfloat16 [16384, 1280], P(('dp', 'mp', 'rep')), may hold values from -64 to 64
- key_rows: bfloat16 [16384, 1280], P(('dp', 'mp', 'rep')), may hold values from -7 to 7
- value_rows: bfloat16 [16384, 1280], P(('dp', 'mp', 'rep')), may hold values from -6 to 6
- residual: bfloat16 [16384, 1280], P(('dp', 'mp', 'rep')), may hold values from -6 to 6
- out_proj: bfloat16 [1280, 1280], replicated, may hold values from -0.15625 to 0.15625
- merge_gain: float32 [1280], replicated, may hold values from 0.1 to 1.9
- merger_proj: bfloat16 [5120, 8192], P(None, ('mp', 'rep')), may hold values from -1.5 to 1.5
- model_gain: float32 [8192], P(('mp', 'rep')), may hold values from 0.1 to 1.9
- image_grid: int32 [1024, 2], replicated, may hold values from 1 to 4, as said below
- image_group: int32 [1024], replicated, may hold values from 0 to 15, as said below
- rollout_image: int32 [16384], P('dp'), may hold values from 0 to 1023, as said below
- cotangent: bfloat16 [65536, 8192], P('dp', ('mp', 'rep')), may hold values from -0.078125 to 0.078125
Outputs:
- normed_tokens: bfloat16 [4096, 8192], P('dp', ('mp', 'rep'))
- merger_grad: float32 [5120, 8192], P('dp', ('mp', 'rep'))
Inputs may be any that keep to these rules, and one draw needn't show every extreme that they name: `image_grid`: height times width of every image is between 1 and 4; image 0 has height 4 and width 1. `image_group`: every rollout group receives exactly 64 images. Among the 64 images of one owner group (images k * 64 to k * 64 + 63) at most 5 go to any one rollout group, and every owner group sends exactly 5 to some rollout group. `rollout_image`: rollouts come in blocks of 1024, one block a rollout group in order of group; every image has exactly 16 rollouts, all in the block of its image_group.
All inputs are finite; a program needn't handle non-finite values.
Results may differ from a plain program's by a relative error of at most 0.02.
Values may be sent and summed in bfloat16 or wider, within the bound.
A program may use at most 64 MiB of HBM per device.

v0:
```python
import functools

import jax
import jax.numpy as jnp
from jax import lax
from jax.sharding import PartitionSpec as P

HEADS = 16
D = 8192


EPSILON = 1e-06


def one_axis_at_a_time(array, axes):
    return functools.reduce(lax.psum, axes, array)


def laid_out(blocks, dim):
    dims = list(blocks.shape[1:])
    dims[dim] *= blocks.shape[0]
    return jnp.moveaxis(blocks, 0, dim).reshape(dims)


def gather_in_order(array, axes, order):
    blocks = array[None]
    for k in order:
        blocks = lax.all_gather(blocks, axes[k], axis=0, tiled=True)
    carried = [lax.axis_size(axes[k]) for k in reversed(order)]
    blocks = blocks.reshape(*carried, *array.shape)
    turned = sorted(range(len(order)), key=lambda place: order[len(order) - 1 - place])
    return blocks.transpose(*turned, *range(len(order), blocks.ndim)).reshape(-1, *array.shape)


def gather_axes(array, axes, order, dim):
    return laid_out(gather_in_order(array, axes, order), dim)


def cut_along(array, dim, count):
    dims = array.shape
    blocks = array.reshape(*dims[:dim], count, dims[dim] // count, *dims[dim + 1 :])
    return jnp.moveaxis(blocks, dim, 0)


def sent_and_summed(array, axis, dim):
    blocks = cut_along(array, dim, lax.axis_size(axis))
    arrived = lax.all_to_all(blocks, axis, split_axis=0, concat_axis=0, tiled=True)
    return arrived.astype(jnp.float32).sum(axis=0)


def attend(query_rows, key_rows, value_rows, valid_count):
    slot_count = query_rows.shape[0]
    feature_width = query_rows.shape[1]
    head_size = feature_width // HEADS
    query_heads = query_rows.reshape(slot_count, HEADS, head_size)
    key_heads = key_rows.reshape(slot_count, HEADS, head_size)
    value_heads = value_rows.reshape(slot_count, HEADS, head_size)
    scores = jnp.einsum(
        "phd,khd->hpk", query_heads, key_heads, preferred_element_type=jnp.float32
    ) * head_size ** (-0.5)
    key_valid = jnp.arange(slot_count, dtype=jnp.int32) < valid_count
    scores = jnp.where(key_valid[None, None, :], scores, -1e30)
    weights = jax.nn.softmax(scores, axis=-1).astype(jnp.bfloat16)
    attended = jnp.einsum("hpk,khd->phd", weights, value_heads, preferred_element_type=jnp.float32)
    return attended.astype(jnp.bfloat16).reshape(slot_count, feature_width)


def row_total(local_part):
    return one_axis_at_a_time(local_part, ("mp", "rep"))


def on_device(
    query_rows,
    key_rows,
    value_rows,
    residual,
    out_proj,
    merge_gain,
    merger_proj,
    model_gain,
    image_grid,
    image_group,
    rollout_image,
    cotangent,
):
    group_count = lax.axis_size("dp")
    member_count = lax.axis_size("mp") * lax.axis_size("rep")
    capacity = member_count // group_count + 1
    own_image = lax.axis_index(("dp", "mp", "rep"))
    own_group = lax.axis_index("dp")
    counts = image_grid[:, 0] * image_grid[:, 1]
    own_count = lax.dynamic_index_in_dim(counts, own_image, keepdims=False)
    patch_count = query_rows.shape[0]
    token_count = patch_count // 4
    merged_width = 4 * query_rows.shape[1]
    column_count = merger_proj.shape[1]
    row_width = token_count * column_count
    patch_valid = (jnp.arange(patch_count, dtype=jnp.int32) < 4 * own_count).astype(jnp.float32)
    attended = attend(query_rows, key_rows, value_rows, 4 * own_count)
    mixed_rows = residual.astype(jnp.float32) + jnp.dot(
        attended, out_proj, preferred_element_type=jnp.float32
    )
    inverse_rms = lax.rsqrt(jnp.mean(mixed_rows * mixed_rows, axis=-1, keepdims=True) + EPSILON)
    merged = (mixed_rows * inverse_rms * merge_gain * patch_valid[:, None]).astype(jnp.bfloat16)
    merged = merged.reshape(token_count, merged_width)
    row_block = gather_axes(merged, ("mp", "rep"), (0, 1), 0)
    outputs = jnp.dot(row_block, merger_proj, preferred_element_type=jnp.float32).astype(
        jnp.bfloat16
    )
    joined = jnp.concatenate([row_block, outputs], axis=1)
    group_merged = joined[:, :merged_width]
    group_out = joined[:, merged_width:]
    member_index = jnp.arange(member_count, dtype=jnp.int32)
    destinations = image_group.reshape(group_count, member_count)
    earlier = member_index[:, None] > member_index[None, :]
    same_dest = destinations[:, :, None] == destinations[:, None, :]
    dest_ranks = jnp.sum((same_dest & earlier[None]).astype(jnp.int32), axis=2)
    own_dest = lax.dynamic_index_in_dim(destinations, own_group, keepdims=False)
    own_ranks = lax.dynamic_index_in_dim(dest_ranks, own_group, keepdims=False)
    slot_index = jnp.arange(group_count * capacity, dtype=jnp.int32)
    select = (slot_index[:, None] == (own_dest * capacity + own_ranks)[None, :]).astype(
        jnp.bfloat16
    )
    outgoing = jnp.dot(
        select, group_out.reshape(member_count, row_width), preferred_element_type=jnp.float32
    )
    outgoing = outgoing.astype(jnp.bfloat16).reshape(group_count, capacity, row_width)
    incoming = lax.all_to_all(outgoing, "dp", split_axis=0, concat_axis=0, tiled=True)
    arriving = destinations == own_group
    per_source = jnp.sum(arriving.astype(jnp.int32), axis=1)
    offsets = jnp.cumsum(per_source) - per_source
    slot_rank = jnp.arange(capacity, dtype=jnp.int32)[None, :]
    placed = jnp.where(slot_rank < per_source[:, None], offsets[:, None] + slot_rank, -1).reshape(
        -1
    )
    compact = (member_index[:, None] == placed[None, :]).astype(jnp.bfloat16)
    model_rows = jnp.dot(
        compact,
        incoming.reshape(group_count * capacity, row_width),
        preferred_element_type=jnp.float32,
    )
    model_rows = model_rows.astype(jnp.bfloat16)
    image_pos = jnp.where(arriving, offsets[:, None] + dest_ranks, -1).reshape(-1)
    matches = member_index[:, None] == image_pos[None, :]
    image_ids = jnp.arange(image_pos.shape[0], dtype=jnp.int32)
    arrived_ids = jnp.sum(jnp.where(matches, image_ids[None, :], 0), axis=1)
    arrived_counts = jnp.sum(jnp.where(matches, counts[None, :], 0), axis=1)
    assign = rollout_image[None, :] == arrived_ids[:, None]
    token_valid = (
        jnp.arange(token_count, dtype=jnp.int32)[None, :] < arrived_counts[:, None]
    ).astype(jnp.float32)
    hidden = model_rows.reshape(member_count, token_count, column_count).astype(jnp.float32)
    squares = row_total(jnp.sum(hidden * hidden, axis=-1))
    inverse = lax.rsqrt(squares / D + EPSILON)
    normed_tokens = (hidden * inverse[..., None] * model_gain).astype(jnp.bfloat16)
    normed_tokens = normed_tokens.reshape(member_count * token_count, column_count)
    rollout_count = rollout_image.shape[0]
    assign_bf = assign.astype(jnp.bfloat16)
    flat_cot = cotangent.reshape(rollout_count, row_width)
    summed = jnp.dot(assign_bf, flat_cot, preferred_element_type=jnp.float32)
    summed = summed.reshape(member_count, token_count, column_count) * token_valid[..., None]
    inner_sum = row_total(jnp.sum(summed * model_gain * hidden, axis=-1))
    token_grad = (
        inverse[..., None] * model_gain * summed - hidden * (inverse**3 / D * inner_sum)[..., None]
    )
    token_grad = token_grad.astype(jnp.bfloat16).reshape(member_count, row_width)
    back_slots = jnp.dot(compact.T, token_grad, preferred_element_type=jnp.float32)
    back_slots = back_slots.astype(jnp.bfloat16).reshape(group_count, capacity, row_width)
    returned = lax.all_to_all(back_slots, "dp", split_axis=0, concat_axis=0, tiled=True)
    group_grads = jnp.dot(
        select.T,
        returned.reshape(group_count * capacity, row_width),
        preferred_element_type=jnp.float32,
    )
    group_grads = group_grads.astype(jnp.bfloat16).reshape(member_count * token_count, column_count)
    whole_term = lax.dot_general(
        group_merged, group_grads, (((0,), (0,)), ((), ())), preferred_element_type=jnp.float32
    )
    merger_grad = sent_and_summed(whole_term.astype(jnp.bfloat16), "dp", 0)
    return (normed_tokens, merger_grad)


def solution(mesh):
    return jax.shard_map(
        on_device,
        mesh=mesh,
        in_specs=(
            P(("dp", "mp", "rep"), None),
            P(("dp", "mp", "rep"), None),
            P(("dp", "mp", "rep"), None),
            P(("dp", "mp", "rep"), None),
            P(),
            P(),
            P(None, ("mp", "rep")),
            P(("mp", "rep")),
            P(),
            P(),
            P("dp"),
            P("dp", ("mp", "rep")),
        ),
        out_specs=(P("dp", ("mp", "rep")), P("dp", ("mp", "rep"))),
        check_vma=False,
    )
```

profile of v0, /device:TPU:1, one launch (start us, length us, event | category | flops | bytes accessed | tf_op | source)
XLA Modules:
  0.0 239.0 jit_solution(15223701048447833139)
XLA Ops:
  7.2 0.9 slice_multiply_fusion
  9.3 0.9 reshape.210
  10.3 0.9 reshape.211
  11.4 0.8 fusion.3
  12.2 0.9 reshape.212
  13.1 1.2 fusion.5
  14.5 1.4 multiply_reduce_fusion.1
  16.1 32.2 %all_gather.6 = bf16[8,4,5120]{2,1,0:T(4,128)(2,1)S(1)} all-gather(bf16[1,4,5120]{2,1,0:T(4,128)(2,1)S(1)} %broadcast_in_dim_reshape.2), channel_id=1, replica_groups=mesh['dp'=16,'mp'=8,'rep'=8] {'mp'}, dimensions={0}, use_global_device_ids=true | all-gather | bytes 368640 | tf_op jit(solution)/shard_map/all_gather | solution.py:28
  48.3 0.8 copy.97
  50.5 2.5 %reshape.218 = bf16[1024,512]{1,0:T(8,128)(2,1)} reshape(bf16[4096,128]{1,0:T(8,128)(2,1)} %param.23) | data formatting | bytes 2097152 | tf_op jit(solution)/shard_map/reshape | solution.py:159
  53.0 2.3 copy.101
  56.0 42.5 %all-gather.2.cloned.1.call-done = bf16[64,4,5120]{2,0,1:T(8,128)(2,1)} async-done(((bf16[8,4,5120]{2,0,1:T(8,128)(2,1)}), bf16[64,4,5120]{2,0,1:T(8,128)(2,1)}) %all-gather.2.cloned.1.call-update) | async-done | bytes 2621456 | tf_op jit(solution)/shard_map/all_gather | solution.py:28
  98.5 5.3 %copy.98 = bf16[8,8,4,5120]{3,2,1,0:T(4,128)(2,1)} copy(bf16[8,8,4,5120]{3,0,1,2:T(8,128)(2,1)} %bitcast.59) | data formatting | bytes 5242880 | tf_op jit(solution)/shard_map/transpose | solution.py:32
  103.8 5.2 %reshape_reshape.3 = bf16[256,5120]{1,0:T(8,128)(2,1)} reshape(bf16[8,8,4,5120]{3,2,1,0:T(4,128)(2,1)} %copy.98) | data formatting | bytes 5242880 | tf_op jit(solution)/shard_map/reshape;reshape | solution.py:22
  109.0 2.9 %convolution_convert_fusion.5 = bf16[256,128]{1,0:T(8,128)(2,1)S(1)} fusion(bf16[256,5120]{1,0:T(8,128)(2,1)} %reshape_reshape.3, bf16[5120,128]{1,0:T(8,128)(2,1)} %param.18), kind=kOutput, calls=%fused_computation.14 | convolution fusion | flops 335577088 | bytes 3997696 | tf_op jit(solution)/shard_map/dot_general | solution.py:107
  112.9 10.4 %all-to-all-start = ((bf16[16,5,512]{2,1,0:T(8,128)(2,1)}), bf16[16,5,512]{2,1,0:T(8,128)(2,1)S(1)}, u32[]{:S(2)}, u32[]{:S(2)}) async-start(bf16[16,5,512]{2,1,0:T(8,128)(2,1)} %reshape.216), calls=%async_computation | async-start | bytes 262144 | tf_op jit(solution)/shard_map/all_to_all | solution.py:128
  123.3 8.9 %all-to-all-done = bf16[16,5,512]{2,1,0:T(8,128)(2,1)S(1)} async-done(((bf16[16,5,512]{2,1,0:T(8,128)(2,1)}), bf16[16,5,512]{2,1,0:T(8,128)(2,1)S(1)}, u32[]{:S(2)}, u32[]{:S(2)}) %all-to-all-start) | async-done | bytes 81952 | tf_op jit(solution)/shard_map/all_to_all | solution.py:128
  132.5 0.8 multiply_reduce_fusion
  133.2 0.8 copy.99
  134.0 1.8 fusion.10
  135.9 16.2 %all-reduce.1 = (f32[64,4]{0,1:T(4,128)S(1)}, f32[64,4]{0,1:T(4,128)}) all-reduce(f32[64,4]{0,1:T(4,128)S(1)} %copy.99, f32[64,4]{0,1:T(4,128)S(1)} %get-tuple-element.12), channel_id=1, replica_groups=mesh['dp'=16,'mp'=8,'rep'=8] {'mp'}, use_global_device_ids=true, to_apply=%region_7.8 | all-reduce | flops 512 | bytes 4096 | tf_op jit(solution)/shard_map/psum | solution.py:16
  152.1 12.7 %all-reduce = (f32[64,4]{0,1:T(4,128)S(1)}, f32[64,4]{0,1:T(4,128)S(1)}) all-reduce(f32[64,4]{0,1:T(4,128)S(1)} %get-tuple-element.6, f32[64,4]{0,1:T(4,128)} %get-tuple-element.7), channel_id=1, replica_groups=mesh['dp'=16,'mp'=8,'rep'=8] {'rep'}, use_global_device_ids=true, to_apply=%region_8.9 | all-reduce | flops 512 | bytes 4096 | tf_op jit(solution)/shard_map/psum | solution.py:16
  165.3 1.5 convolution_convert_fusion.1
  166.9 0.9 reshape.220
  167.8 19.6 %all_to_all.15 = bf16[16,5,512]{2,1,0:T(8,128)(2,1)} all-to-all(bf16[16,5,512]{2,1,0:T(8,128)(2,1)S(1)} %reshape.220), channel_id=1, replica_groups=mesh['dp'=16,'mp'=8,'rep'=8] {'dp'}, dimensions={0} | all-to-all | bytes 163840 | tf_op jit(solution)/shard_map/all_to_all | solution.py:169
  187.4 0.9 reshape.221
  188.4 0.8 convolution_convert_fusion.3
  189.3 3.7 %convolution_convert_fusion = bf16[5120,128]{1,0:T(8,128)(2,1)} fusion(bf16[256,5120]{1,0:T(8,128)(2,1)} %reshape_reshape.3, bf16[256,128]{1,0:T(8,128)(2,1)S(1)} %reshape.222), kind=kOutput, calls=%fused_computation.1 | convolution fusion | flops 336199680 | bytes 3997696 | tf_op jit(solution)/shard_map/dot_general | solution.py:176
  193.0 4.4 %all-to-all-start.2 = ((bf16[16,320,128]{2,1,0:T(8,128)(2,1)}), bf16[16,320,128]{2,1,0:T(8,128)(2,1)}, u32[]{:S(2)}, u32[]{:S(2)}) async-start(bf16[16,320,128]{2,1,0:T(8,128)(2,1)} %bitcast.56), calls=%async_computation.2 | async-start | bytes 2621440 | tf_op jit(solution)/shard_map/all_to_all | solution.py:47
  197.7 0.7 multiply_convert_fusion
  198.4 31.6 %all-to-all-done.2 = bf16[16,320,128]{2,1,0:T(8,128)(2,1)} async-done(((bf16[16,320,128]{2,1,0:T(8,128)(2,1)}), bf16[16,320,128]{2,1,0:T(8,128)(2,1)}, u32[]{:S(2)}, u32[]{:S(2)}) %all-to-all-start.2) | async-done | bytes 1310752 | tf_op jit(solution)/shard_map/all_to_all | solution.py:47
  230.0 2.2 convert_reduce_fusion
  (55 shorter events, 5.8 us)
Async XLA Ops:
  7.2 7.3 %copy-start = (bf16[1280,1280]{1,0:T(8,128)(2,1)S(1)}, bf16[1280,1280]{1,0:T(8,128)(2,1)}, u32[]{:S(2)}) copy-start(bf16[1280,1280]{1,0:T(8,128)(2,1)} %param.16) | copy-start | bytes 9830404
  7.2 91.3 %all-gather.2.cloned.1.call-start = ((), (), s32[]{:S(2)}) async-start(), calls=%async_computation.3 | async-start | bytes 2949120 | tf_op jit(solution)/shard_map/all_gather | solution.py:28
  11.2 4.8 %copy-start.4 = (f32[1280]{0:T(1024)S(1)}, f32[1280]{0:T(1024)}, u32[]{:S(2)}) copy-start(f32[1280]{0:T(1024)} %param.17) | copy-start | bytes 15364
  14.3 34.8 %copy-start.3 = (s32[1024]{0:T(1024)S(1)}, s32[1024]{0:T(1024)}, u32[]{:S(2)}) copy-start(s32[1024]{0:T(1024)} %param.21) | copy-start | bytes 12292
  49.8 82.5 %copy-start.7 = (s32[80]{0:T(128)}, s32[80]{0:T(128)S(1)}, u32[]{:S(2)}) copy-start(s32[80]{0:T(128)S(1)} %select_n.38) | copy-start | bytes 964
  55.2 56.8 %copy-start.8 = (s32[64]{0:T(128)}, s32[64]{0:T(128)S(1)}, u32[]{:S(2)}) copy-start(s32[64]{0:T(128)S(1)} %fusion.30) | copy-start | bytes 772
  109.0 25.0 %copy-start.5 = (f32[128]{0:T(128)S(1)}, f32[128]{0:T(128)}, u32[]{:S(2)}) copy-start(f32[128]{0:T(128)} %param.19) | copy-start | bytes 1540
  112.9 19.3 %all-to-all-start = ((bf16[16,5,512]{2,1,0:T(8,128)(2,1)}), bf16[16,5,512]{2,1,0:T(8,128)(2,1)S(1)}, u32[]{:S(2)}, u32[]{:S(2)}) async-start(bf16[16,5,512]{2,1,0:T(8,128)(2,1)} %reshape.216), calls=%async_computation | async-start | bytes 262144 | tf_op jit(solution)/shard_map/all_to_all | solution.py:128
  164.7 0.6 copy-start.1
  193.0 4.4 %copy-start.2 = (f32[64,4]{0,1:T(4,128)S(1)}, f32[64,4]{0,1:T(4,128)}, u32[]{:S(2)}) copy-start(f32[64,4]{0,1:T(4,128)} %copy-done.1) | copy-start | bytes 3076
  193.0 4.7 %copy-start.6 = (f32[128]{0:T(128)S(1)}, f32[128]{0:T(128)}, u32[]{:S(2)}) copy-start(f32[128]{0:T(128)} %param.19) | copy-start | bytes 1540
  193.0 37.0 %all-to-all-start.2 = ((bf16[16,320,128]{2,1,0:T(8,128)(2,1)}), bf16[16,320,128]{2,1,0:T(8,128)(2,1)}, u32[]{:S(2)}, u32[]{:S(2)}) async-start(bf16[16,320,128]{2,1,0:T(8,128)(2,1)} %bitcast.56), calls=%async_computation.2 | async-start | bytes 2621440 | tf_op jit(solution)/shard_map/all_to_all | solution.py:47
Sparse Core Ops, SparseCore 0:
  49.3 49.1 all-gather.1
where the time goes:
time: 240 us; the launch traced here: 239 us
  waiting for transfers between devices  83 us (35%)
  blocking collectives  80.7 us (34%)
  local copies, waits for them, and re-layouts  23.7 us (10%)
  starting transfers between devices  14.9 us (6%)
  matrix products  14.8 us (6%)
  between operations  14.3 us (6%)
  other arithmetic  7.55 us (3%)
    all_gather x1, waiting for transfers between devices, gather_in_order(): blocks = lax.all_gather(blocks, axes[k], axis=0, tiled=True)  42.5 us
    all_gather x1, blocking collectives, gather_in_order(): blocks = lax.all_gather(blocks, axes[k], axis=0, tiled=True)  32.2 us
    all_to_all x1, waiting for transfers between devices, sent_and_summed(): lax.all_to_all(blocks, axis, split_axis=0, concat_axis=0, tiled=True)  31.6 us
    psum x2, blocking collectives, one_axis_at_a_time(): return functools.reduce(lax.psum, axes, array)  28.9 us
    all_to_all x1, blocking collectives, on_device(): lax.all_to_all(back_slots, 'dp', split_axis=0, concat_axis=0, tiled=True)  19.6 us
    all_to_all x1, starting transfers between devices, on_device(): lax.all_to_all(outgoing, 'dp', split_axis=0, concat_axis=0, tiled=True)  10.4 us
    all_to_all x1, waiting for transfers between devices, on_device(): lax.all_to_all(outgoing, 'dp', split_axis=0, concat_axis=0, tiled=True)  8.88 us
    transpose x1, local copies, waits for them, and re-layouts, gather_in_order(): blocks.transpose(*turned, *range(len(order), blocks.ndim))  5.29 us
  transfers between devices with their start and end apart: 3, of which 3 were waited for; matrix products, arithmetic and copies ran while one was open for 3% of the time, Pallas kernels for 0%

commit v1 on v0

v1 whole, which is shorter than its diff:
```python
import functools

import jax
import jax.numpy as jnp
from jax import lax
from jax.experimental import pallas as pl
from jax.experimental.pallas import tpu as pltpu
from jax.sharding import PartitionSpec as P

HEADS = 16
HEAD = 80
DV = 1280
D = 8192
EPSILON = 1e-06
RING = 8
GROUPS = 16
MEMBERS = 64
SLOTS = 16
ROWS = MEMBERS * SLOTS
TOKENS = MEMBERS * 4
HALF = DV // 2
COLS = 128
BLOCK = 32
ROUTED = GROUPS * BLOCK
PIECE = 320
MESH = pl.DeviceIdType.MESH
F32 = jnp.float32
BF16 = jnp.bfloat16


def iota(shape, dim):
    return lax.broadcasted_iota(jnp.int32, shape, dim)


def dot(a, b):
    return jnp.dot(a, b, preferred_element_type=F32)


def dot_first(a, b):
    return lax.dot_general(a, b, (((0,), (0,)), ((), ())), preferred_element_type=F32)


def remote(src, dst, send, recv, device):
    return pltpu.make_async_remote_copy(
        src_ref=src,
        dst_ref=dst,
        send_sem=send,
        recv_sem=recv,
        device_id=device,
        device_id_type=MESH,
    )


def kernel(
    q_hbm,
    k_hbm,
    v_hbm,
    res_hbm,
    wo_hbm,
    merge_gain_ref,
    w_hbm,
    gain_ref,
    grid_ref,
    group_ref,
    roll_ref,
    cot_hbm,
    normed_out,
    grad_out,
    q_buf,
    k_buf,
    v_buf,
    res_buf,
    wo_buf,
    w_buf,
    cot_buf,
    own_buf,
    rows,
    rows_t,
    wide,
    spread,
    row_key,
    pos_key,
    col_key,
    sums,
    sum_out,
    sum_in,
    pick,
    hidden_buf,
    packet,
    z_in,
    y_in,
    norm_out,
    norm_in,
    kept,
    pair_out,
    pair_in,
    chain_out,
    chain_in,
    load_sem,
    gather_send,
    gather_recv,
    sum_send,
    sum_recv,
    stat_send,
    z_recv,
    y_recv,
    norm_send,
    norm_recv,
    pair_send,
    pair_recv,
    chain_send,
    chain_recv,
):
    d = lax.axis_index("dp")
    z = lax.axis_index("mp")
    y = lax.axis_index("rep")
    x = d // 2
    core = d % 2

    loads = [
        pltpu.make_async_copy(q_hbm, q_buf, load_sem.at[0]),
        pltpu.make_async_copy(k_hbm, k_buf, load_sem.at[1]),
        pltpu.make_async_copy(v_hbm, v_buf, load_sem.at[2]),
        pltpu.make_async_copy(res_hbm, res_buf, load_sem.at[3]),
        pltpu.make_async_copy(wo_hbm, wo_buf, load_sem.at[4]),
        pltpu.make_async_copy(cot_hbm, cot_buf, load_sem.at[5]),
    ] + [
        pltpu.make_async_copy(
            w_hbm.at[pl.ds(j * DV, DV), :], w_buf.at[:, pl.ds(j * COLS, COLS)], load_sem.at[6 + j]
        )
        for j in range(4)
    ]
    for load in loads:
        load.start()

    barrier = pltpu.get_barrier_semaphore()

    def greet(axis, me, size):
        def step(i, carry):
            pl.semaphore_signal(
                barrier, inc=1, device_id={axis: (me + i) % size}, device_id_type=MESH
            )
            return carry

        lax.fori_loop(1, size, step, 0)

    greet("mp", z, RING)
    greet("rep", y, RING)
    greet("dp", d, GROUPS)

    factors = grid_ref[...]
    products = factors[0:1, :] * factors[1:2, :]
    counts = jnp.concatenate(
        [products[:, 128 * a : 128 * a + 128] for a in range(8)], axis=0
    ).astype(F32)
    sub8 = iota((8, 128), 0)
    lane8 = iota((8, 128), 1)
    own_image = d * MEMBERS + z * RING + y
    is_own = (sub8 == own_image // 128) & (lane8 == own_image % 128)
    own_count = jnp.sum(
        jnp.sum(jnp.where(is_own, counts, 0.0), axis=0, keepdims=True), axis=1, keepdims=True
    )
    own_valid = own_count * 4.0

    loads[0].wait()
    loads[1].wait()
    head_of_row = iota((256, DV), 0) // SLOTS
    feature = iota((256, DV), 1)
    in_head = (feature >= head_of_row * HEAD) & (feature < head_of_row * HEAD + HEAD)
    queries = jnp.concatenate([q_buf[...].astype(F32)] * HEADS, axis=0)
    queries = jnp.where(in_head, queries, 0.0).astype(BF16)
    scores = lax.dot_general(
        queries, k_buf[...], (((1,), (1,)), ((), ())), preferred_element_type=F32
    ) * HEAD ** (-0.5)
    key_slot = iota((256, SLOTS), 1).astype(F32)
    scores = jnp.where(key_slot < own_valid, scores, -1e30)
    top = jnp.max(scores, axis=1, keepdims=True)
    powers = jnp.exp(scores - top)
    weights = (powers / jnp.sum(powers, axis=1, keepdims=True)).astype(BF16)
    loads[2].wait()
    attended = jnp.where(in_head, dot(weights, v_buf[...]), 0.0)
    attended = jnp.sum(attended.reshape(HEADS, SLOTS, DV), axis=0).astype(BF16)
    loads[3].wait()
    loads[4].wait()
    mixed = res_buf[...].astype(F32) + dot(attended, wo_buf[...])
    inverse_rms = lax.rsqrt(jnp.sum(mixed * mixed, axis=1, keepdims=True) / DV + EPSILON)
    slot_valid = (iota((SLOTS, 1), 0).astype(F32) < own_valid).astype(F32)
    own_buf[...] = (mixed * inverse_rms * merge_gain_ref[...] * slot_valid).astype(BF16)

    def image_rows(zz, yy):
        return pl.ds(pl.multiple_of((zz * RING + yy) * SLOTS, SLOTS), SLOTS)

    def half_of(half, zz, yy):
        return rows.at[image_rows(zz, yy), pl.ds(half * HALF, HALF)]

    pl.semaphore_wait(barrier, 2 * (RING - 1) + GROUPS - 1)

    def push(half, src, zz, yy, device):
        remote(
            src,
            half_of(half, zz, yy),
            gather_send.at[half],
            gather_recv.at[half, zz * RING + yy],
            device,
        ).start()

    def arrive(half, zz, yy):
        ref = half_of(half, zz, yy)
        remote(
            ref,
            ref,
            gather_send.at[half],
            gather_recv.at[half, zz * RING + yy],
            {"rep": (y + 1) % RING},
        ).wait_recv()

    up_y, down_y = {"rep": (y + 1) % RING}, {"rep": (y + RING - 1) % RING}
    up_z, down_z = {"mp": (z + 1) % RING}, {"mp": (z + RING - 1) % RING}
    own0 = own_buf.at[:, pl.ds(0, HALF)]
    own1 = own_buf.at[:, pl.ds(HALF, HALF)]

    def shift(o):
        return (1 - 2 * (o % 2)) * ((o + 1) // 2)

    push(0, own0, z, y, up_y)
    push(0, own0, z, y, down_y)
    push(1, own1, z, y, up_z)
    push(1, own1, z, y, down_z)

    def spread_own(o, carry):
        push(0, own0, z, y, {"mp": (z + RING + shift(o)) % RING})
        push(1, own1, z, y, {"rep": (y + RING + shift(o)) % RING})
        return carry

    lax.fori_loop(1, RING, spread_own, 0)
    rows[image_rows(z, y), :] = own_buf[...]

    groups = group_ref[...]
    arriving = groups == d
    arrived = arriving.astype(F32).astype(BF16)
    before = iota((128, 128), 0)
    after = iota((128, 128), 1)
    earlier = before < after
    rank_in_owner = dot(
        arrived, (earlier & (before // MEMBERS == after // MEMBERS)).astype(F32).astype(BF16)
    )
    rank_in_chunk = dot(arrived, earlier.astype(F32).astype(BF16))
    lower = (iota((8, 8), 0) > iota((8, 8), 1)).astype(F32).astype(BF16)
    chunk_start = jnp.sum(dot(lower, arrived), axis=1, keepdims=True)
    place = rank_in_chunk + chunk_start
    slot_in_chunk = jnp.where(
        arriving, (lane8 // MEMBERS).astype(F32) * 8.0 + rank_in_owner, -1.0
    )
    image_key = (sub8 * 128 + lane8).astype(F32) * 4.0
    slot_of_row = (iota((64, 128), 0) // 4).astype(F32)
    token_of_row = (iota((64, 1), 0) % 4).astype(F32)
    for a in range(8):
        match = slot_in_chunk[a : a + 1, :] == slot_of_row

        def total(value):
            return jnp.sum(jnp.where(match, value[a : a + 1, :], 0.0), axis=1, keepdims=True)

        found = total(counts)
        row_key[64 * a : 64 * a + 64, :] = jnp.where(
            token_of_row < found, total(image_key) + token_of_row, -1.0
        )
        pos_key[64 * a : 64 * a + 64, :] = jnp.where(
            found > 0.0, total(place) * 4.0 + token_of_row, -1.0
        )
    rollouts = roll_ref[...]
    widen = (iota((128, 512), 0) == iota((128, 512), 1) // 4).astype(F32).astype(BF16)
    high = dot((rollouts // 32).astype(F32).astype(BF16), widen)
    low = dot((rollouts % 32).astype(F32).astype(BF16), widen)
    col_key[...] = (high * 32.0 + low) * 4.0 + (iota((8, 512), 1) % 4).astype(F32)
    sums[...] = jnp.zeros_like(sums)
    loads[5].wait()

    def add_chunk(a):
        chosen = (row_key[...] == col_key[pl.ds(a, 1), :]).astype(F32).astype(BF16)
        part = cot_buf[pl.ds(pl.multiple_of(a * 512, 512), 512), :]
        sums[...] += dot(chosen, part)

    add_chunk(0)

    def first_axis(o, carry):
        zz = (z + RING + shift(o)) % RING
        yy = (y + RING + shift(o)) % RING
        arrive(0, zz, y)
        push(0, half_of(0, zz, y), zz, y, up_y)
        push(0, half_of(0, zz, y), zz, y, down_y)
        arrive(1, z, yy)
        push(1, half_of(1, z, yy), z, yy, up_z)
        push(1, half_of(1, z, yy), z, yy, down_z)
        add_chunk(o)
        return carry

    lax.fori_loop(1, RING, first_axis, 0)

    sum_out[...] = sums[...].astype(BF16)

    def routed(buf, peer):
        return buf.at[pl.ds(pl.multiple_of(peer * BLOCK, BLOCK), BLOCK), :]

    def exchange(out_buf, in_buf, send, recv):
        def step(i, carry):
            peer = (d + i) % GROUPS
            remote(
                routed(out_buf, peer), routed(in_buf, d), send, recv.at[d], {"dp": peer}
            ).start()
            return carry

        lax.fori_loop(1, GROUPS, step, 0)
        here = pl.ds(pl.multiple_of(d * BLOCK, BLOCK), BLOCK)
        in_buf[here, :] = out_buf[here, :]

    def exchanged(out_buf, in_buf, send, recv):
        def step(i, carry):
            peer = (d + i) % GROUPS
            remote(
                routed(out_buf, peer), routed(in_buf, peer), send, recv.at[peer], {"dp": peer}
            ).wait_recv()
            return carry

        lax.fori_loop(1, GROUPS, step, 0)

    exchange(sum_out, sum_in, sum_send, sum_recv)

    def hop(h, o, up, down):
        zz = (z + RING + shift(o)) % RING
        yy = (y + RING + shift(o)) % RING
        below, above = (y + RING - h) % RING, (y + h) % RING
        arrive(0, zz, below)
        if up:
            push(0, half_of(0, zz, below), zz, below, up_y)
        arrive(0, zz, above)
        if down:
            push(0, half_of(0, zz, above), zz, above, down_y)
        below, above = (z + RING - h) % RING, (z + h) % RING
        arrive(1, below, yy)
        if up:
            push(1, half_of(1, below, yy), below, yy, up_z)
        arrive(1, above, yy)
        if down:
            push(1, half_of(1, above, yy), above, yy, down_z)

    def near_hops(i, carry):
        hop(i // RING + 1, i % RING, True, True)
        return carry

    lax.fori_loop(0, 2 * RING, near_hops, 0)

    def third_hop(i, carry):
        hop(3, 2 * i, True, False)
        hop(3, 2 * i + 1, False, True)
        return carry

    lax.fori_loop(0, RING // 2, third_hop, 0)

    own_half = (d % 2) * MEMBERS
    own_dest = jnp.sum(
        jnp.where(sub8 == d // 2, groups.astype(F32), 0.0), axis=0, keepdims=True
    )
    lane = iota((TOKENS, 128), 1)
    own_lane = own_half + iota((TOKENS, 128), 0) // 4
    dest = jnp.sum(jnp.where(lane == own_lane, own_dest, 0.0), axis=1, keepdims=True)
    same = (own_dest == dest) & (lane >= own_half) & (lane < own_lane)
    rank = jnp.sum(jnp.where(same, 1.0, 0.0), axis=1, keepdims=True)
    token = (iota((TOKENS, 1), 0) % 4).astype(F32)
    slot_row = dest * BLOCK + rank * 4.0 + token
    pick[...] = (slot_row == iota((TOKENS, ROUTED), 1).astype(F32)).astype(F32).astype(BF16)
    for load in loads[6:]:
        load.wait()

    def last_hop(o, carry):
        arrive(0, (z + RING + shift(o)) % RING, (y + 4) % RING)
        arrive(1, (z + 4) % RING, (y + RING + shift(o)) % RING)
        return carry

    lax.fori_loop(0, RING, last_hop, 0)

    def project(b, carry):
        here = pl.ds(pl.multiple_of(b * 128, 128), 128)
        product = dot(rows[here, :], w_buf[...])
        for j in range(4):
            wide[j, here, :] = product[:, j * COLS : (j + 1) * COLS]
        return carry

    lax.fori_loop(0, ROWS // 128, project, 0)
    outputs = wide[0, pl.ds(0, TOKENS, stride=4), :]
    for j in range(1, 4):
        outputs += wide[j, pl.ds(j, TOKENS, stride=4), :]
    hidden = outputs.astype(BF16).astype(F32)
    hidden_buf[...] = hidden
    gain = gain_ref[...]
    exchanged(sum_out, sum_in, sum_send, sum_recv)
    summed = dot(pick[...], sum_in[...])
    sums[0:TOKENS, :] = summed
    squares = jnp.sum((hidden * hidden).T, axis=0, keepdims=True)
    inner = jnp.sum((summed * gain * hidden).T, axis=0, keepdims=True)
    packet[0] = jnp.concatenate(
        [
            squares[:, 0:128],
            squares[:, 128:256],
            inner[:, 0:128],
            inner[:, 128:256],
            jnp.zeros((4, 128), F32),
        ],
        axis=0,
    )

    def share(slot, axis, me, in_buf, recv):
        def step(i, carry):
            remote(
                packet.at[slot],
                in_buf.at[me],
                stat_send.at[slot],
                recv.at[me],
                {axis: (me + i) % RING},
            ).start()
            return carry

        lax.fori_loop(1, RING, step, 0)
        in_buf[me] = packet[slot]

    def shared(slot, axis, me, in_buf, recv):
        def step(i, carry):
            peer = (me + i) % RING
            remote(
                packet.at[slot], in_buf.at[peer], stat_send.at[slot], recv.at[peer], {axis: peer}
            ).wait_recv()
            return carry

        lax.fori_loop(1, RING, step, 0)
        return jnp.sum(in_buf[...], axis=0)

    def turn(b, carry):
        here = pl.ds(pl.multiple_of(b * 128, 128), 128)
        rows_t[:, here] = rows[here, :].T
        return carry

    share(0, "mp", z, z_in, z_recv)
    lax.fori_loop(0, 4, turn, 0)
    packet[1] = shared(0, "mp", z, z_in, z_recv)
    share(1, "rep", y, y_in, y_recv)
    lax.fori_loop(4, 8, turn, 0)
    wide[...] = jnp.zeros_like(wide)
    totals = shared(1, "rep", y, y_in, y_recv)

    inverse_row = lax.rsqrt(totals[0:2, :] / D + EPSILON)
    scale_row = inverse_row * inverse_row * inverse_row / D * totals[2:4, :]
    turned = jnp.concatenate([inverse_row, scale_row, jnp.zeros((124, 128), F32)], axis=0).T
    inverse = jnp.concatenate([turned[:, 0:1], turned[:, 1:2]], axis=0)
    scale = jnp.concatenate([turned[:, 2:3], turned[:, 3:4]], axis=0)
    hidden = hidden_buf[...]
    token_grad = (inverse * gain * sums[0:TOKENS, :] - hidden * scale).astype(BF16).astype(F32)
    for j in range(4):
        wide[j, pl.ds(j, TOKENS, stride=4), :] = token_grad
    normed = (hidden * inverse * gain).astype(BF16)

    def narrow(b, carry):
        here = pl.ds(pl.multiple_of(b * 128, 128), 128)
        for j in range(4):
            spread[here, j * COLS : (j + 1) * COLS] = wide[j, here, :].astype(BF16)
        return carry

    lax.fori_loop(0, ROWS // 128, narrow, 0)

    partner = {"dp": 2 * x + 1 - core}

    def for_partner(i, carry):
        first = pl.multiple_of((1 - core + 2 * i) * PIECE, 64)
        here = pl.ds(pl.multiple_of(i * PIECE, 64), PIECE)
        pair_out[here, :] = dot(rows_t[pl.ds(first, PIECE), :], spread[...]).astype(BF16)
        remote(
            pair_out.at[here, :],
            pair_in.at[here, :],
            pair_send.at[i],
            pair_recv.at[i],
            partner,
        ).start()
        return carry

    lax.fori_loop(0, 2, for_partner, 0)

    def for_self(i, carry):
        first = pl.multiple_of((core + 2 * i) * PIECE, 64)
        here = pl.ds(pl.multiple_of(i * PIECE, 64), PIECE)
        kept[here, :] = dot(rows_t[pl.ds(first, PIECE), :], spread[...])
        return carry

    lax.fori_loop(0, 2, for_self, 0)

    def pair_arrived(i, carry):
        here = pl.ds(pl.multiple_of(i * PIECE, 64), PIECE)
        remote(
            pair_out.at[here, :], pair_in.at[here, :], pair_send.at[i], pair_recv.at[i], partner
        ).wait_recv()
        kept[here, :] = kept[here, :] + pair_in[here, :].astype(F32)
        return carry

    lax.fori_loop(0, 2, pair_arrived, 0)

    part = PIECE // 2
    ways = ((0, 1), (1, -1))

    def reach(way, half):
        return 4 if way == half else 3

    def kept_block(chip, half):
        first = pl.multiple_of((chip % 2) * PIECE + half * part, 32)
        return kept[pl.ds(first, part), pl.ds(pl.multiple_of((chip // 2) * COLS, COLS), COLS)]

    def chain(way, sign, half, step):
        return remote(
            chain_out.at[way, half, step],
            chain_in.at[way, half, step],
            chain_send.at[way, half, step],
            chain_recv.at[way, half, step],
            {"dp": 2 * ((x + RING + sign) % RING) + core},
        )

    for step in range(4):
        for half in range(2):
            for way, sign in ways:
                far = reach(way, half)
                if step >= far:
                    continue
                value = kept_block((x + RING + sign * (far - step)) % RING, half)
                if step:
                    chain(way, sign, half, step - 1).wait_recv()
                    value = value + chain_in[way, half, step - 1].astype(F32)
                chain_out[way, half, step] = value.astype(BF16)
                chain(way, sign, half, step).start()
        if step == 0:
            norm_out[...] = dot_first(pick[...], normed).astype(BF16)
            exchange(norm_out, norm_in, norm_send, norm_recv)

    exchanged(norm_out, norm_in, norm_send, norm_recv)
    home = (pos_key[...] == iota((ROUTED, TOKENS), 1).astype(F32)).astype(F32).astype(BF16)
    normed_out[...] = dot_first(home, norm_in[...]).astype(BF16)

    for half in range(2):
        value = kept_block(x, half)
        for way, sign in ways:
            last = reach(way, half) - 1
            chain(way, sign, half, last).wait_recv()
            value = value + chain_in[way, half, last].astype(F32)
        grad_out[half * part : (half + 1) * part, :] = value

    for half in range(2):
        sent = rows.at[pl.ds(0, (MEMBERS - 1) * SLOTS), pl.ds(half * HALF, HALF)]
        remote(
            sent, sent, gather_send.at[half], gather_recv.at[half, 0], {"rep": (y + 1) % RING}
        ).wait_send()
    sent = pl.ds(0, (GROUPS - 1) * BLOCK)
    for out_buf, send, recv in ((sum_out, sum_send, sum_recv), (norm_out, norm_send, norm_recv)):
        remote(
            out_buf.at[sent, :], out_buf.at[sent, :], send, recv.at[0], {"dp": (d + 1) % GROUPS}
        ).wait_send()
    sent = pl.ds(0, RING - 1)
    for slot, in_buf, recv in ((0, z_in, z_recv), (1, y_in, y_recv)):
        remote(
            in_buf.at[sent], in_buf.at[sent], stat_send.at[slot], recv.at[0], {"mp": (z + 1) % RING}
        ).wait_send()
    for i in range(2):
        here = pl.ds(i * PIECE, PIECE)
        remote(
            pair_out.at[here, :], pair_in.at[here, :], pair_send.at[i], pair_recv.at[i], partner
        ).wait_send()
    for half in range(2):
        for way, sign in ways:
            for step in range(reach(way, half)):
                chain(way, sign, half, step).wait_send()


def on_device(
    query_rows,
    key_rows,
    value_rows,
    residual,
    out_proj,
    merge_gain,
    merger_proj,
    model_gain,
    image_grid,
    image_group,
    rollout_image,
    cotangent,
):
    hbm = pl.BlockSpec(memory_space=pl.ANY)
    vmem = pl.BlockSpec(memory_space=pltpu.VMEM)
    dma = pltpu.SemaphoreType.DMA
    part = PIECE // 2
    return pl.pallas_call(
        kernel,
        out_shape=(
            jax.ShapeDtypeStruct((TOKENS, COLS), BF16),
            jax.ShapeDtypeStruct((PIECE, COLS), F32),
        ),
        in_specs=[hbm, hbm, hbm, hbm, hbm, vmem, hbm, vmem, vmem, vmem, vmem, hbm],
        out_specs=(vmem, vmem),
        scratch_shapes=[
            pltpu.VMEM((SLOTS, DV), BF16),
            pltpu.VMEM((SLOTS, DV), BF16),
            pltpu.VMEM((SLOTS, DV), BF16),
            pltpu.VMEM((SLOTS, DV), BF16),
            pltpu.VMEM((DV, DV), BF16),
            pltpu.VMEM((DV, 4 * COLS), BF16),
            pltpu.VMEM((4096, COLS), BF16),
            pltpu.VMEM((SLOTS, DV), BF16),
            pltpu.VMEM((ROWS, DV), BF16),
            pltpu.VMEM((DV, ROWS), BF16),
            pltpu.VMEM((4, ROWS, COLS), F32),
            pltpu.VMEM((ROWS, 4 * COLS), BF16),
            pltpu.VMEM((ROUTED, 1), F32),
            pltpu.VMEM((ROUTED, 1), F32),
            pltpu.VMEM((8, 512), F32),
            pltpu.VMEM((ROUTED, COLS), F32),
            pltpu.VMEM((ROUTED, COLS), BF16),
            pltpu.VMEM((ROUTED, COLS), BF16),
            pltpu.VMEM((TOKENS, ROUTED), BF16),
            pltpu.VMEM((TOKENS, COLS), F32),
            pltpu.VMEM((2, 8, 128), F32),
            pltpu.VMEM((RING, 8, 128), F32),
            pltpu.VMEM((RING, 8, 128), F32),
            pltpu.VMEM((ROUTED, COLS), BF16),
            pltpu.VMEM((ROUTED, COLS), BF16),
            pltpu.VMEM((2 * PIECE, 4 * COLS), F32),
            pltpu.VMEM((2 * PIECE, 4 * COLS), BF16),
            pltpu.VMEM((2 * PIECE, 4 * COLS), BF16),
            pltpu.VMEM((2, 2, 4, part, COLS), BF16),
            pltpu.VMEM((2, 2, 4, part, COLS), BF16),
            dma((10,)),
            dma((2,)),
            dma((2, MEMBERS)),
            dma,
            dma((GROUPS,)),
            dma((2,)),
            dma((RING,)),
            dma((RING,)),
            dma,
            dma((GROUPS,)),
            dma((2,)),
            dma((2,)),
            dma((2, 2, 4)),
            dma((2, 2, 4)),
        ],
        compiler_params=pltpu.CompilerParams(collective_id=0, has_side_effects=True),
        name="merge_step",
    )(
        query_rows,
        key_rows,
        value_rows,
        residual,
        out_proj,
        merge_gain.reshape(1, DV),
        merger_proj,
        model_gain.reshape(1, COLS),
        image_grid.T,
        image_group.reshape(8, 128),
        rollout_image.reshape(8, 128),
        cotangent,
    )


def solution(mesh):
    return jax.shard_map(
        on_device,
        mesh=mesh,
        in_specs=(
            P(("dp", "mp", "rep"), None),
            P(("dp", "mp", "rep"), None),
            P(("dp", "mp", "rep"), None),
            P(("dp", "mp", "rep"), None),
            P(),
            P(),
            P(None, ("mp", "rep")),
            P(("mp", "rep")),
            P(),
            P(),
            P("dp"),
            P("dp", ("mp", "rep")),
        ),
        out_specs=(P("dp", ("mp", "rep")), P("dp", ("mp", "rep"))),
        check_vma=False,
    )
```

time: 240 us -> 83.5 us (0.35)
  waiting for transfers between devices: 83 us -> 0 us
  blocking collectives: 80.7 us -> 0 us
  Pallas kernels: 0 us -> 77.5 us
  local copies, waits for them, and re-layouts: 23.7 us -> 4.36 us
  starting transfers between devices: 14.9 us -> 0 us
  matrix products: 14.8 us -> 0 us
  between operations: 14.3 us -> 0.64 us
  other arithmetic: 7.55 us -> 0 us
    pallas_call x0 -> x1, Pallas kernels: none -> 77.5 us  [on_device(): pl.pallas_call(kernel, out_shape=(jax.ShapeDtypeStruct((TOKENS, COLS), BF...]
    all_gather x1 -> x0, waiting for transfers between devices: 42.5 us -> none  [gather_in_order(): blocks = lax.all_gather(blocks, axes[k], axis=0, tiled=True)]
    all_to_all x2 -> x0, waiting for transfers between devices: 40.5 us -> none  [the longest x1 31.6 us: sent_and_summed(): lax.all_to_all(blocks, axis, split_axis=0, concat_axis=0, tiled=True)]
    all_gather x1 -> x0, blocking collectives: 32.2 us -> none  [gather_in_order(): blocks = lax.all_gather(blocks, axes[k], axis=0, tiled=True)]
    psum x2 -> x0, blocking collectives: 28.9 us -> none  [one_axis_at_a_time(): return functools.reduce(lax.psum, axes, array)]
    all_to_all x1 -> x0, blocking collectives: 19.6 us -> none  [on_device(): lax.all_to_all(back_slots, 'dp', split_axis=0, concat_axis=0, tiled=True)]
    all_to_all x2 -> x0, starting transfers between devices: 14.8 us -> none  [the longest x1 10.4 us: on_device(): lax.all_to_all(outgoing, 'dp', split_axis=0, concat_axis=0, tiled=True)]
    dot_general x10 -> x0, matrix products: 14.6 us -> none  [the longest x1 3.72 us: on_device(): lax.dot_general(group_merged, group_grads, (((0,), (0,)), ((), ())), pref...]
  transfers between devices with their start and end apart: 3 -> 0, of which waited for: 3 -> 0; matrix products, arithmetic and copies ran while one was open for 3% -> 0% of each run, Pallas kernels for 0% -> 0%
where the time goes in v1:
time: 83.5 us; the launch traced here: 82.5 us
  Pallas kernels  77.5 us (93%)
  local copies, waits for them, and re-layouts  4.36 us (5%)
    pallas_call x1, Pallas kernels, on_device(): pl.pallas_call(kernel, out_shape=(jax.ShapeDtypeStruct((TOKENS, COLS), BF...  77.5 us
    unnamed x2, local copies, waits for them, and re-layouts  3.07 us

profile of v1, /device:TPU:1, one launch (start us, length us, event | category | flops | bytes accessed | tf_op | source)
XLA Modules:
  0.0 82.5 jit_solution(13838212157094001002)
XLA Ops:
  0.6 1.3 %reshape.16.merge_gain_ref = f32[1,1280]{1,0:T(1,128)} reshape(f32[1280]{0:T(1024)} %param.17) | data formatting | bytes 10240 | tf_op jit(solution)/shard_map/reshape | solution.py:656
  1.9 77.5 %merge_step.1 = (bf16[256,128]{1,0:T(8,128)(2,1)}, f32[320,128]{1,0:T(8,128)}) custom-call(bf16[16,1280]{1,0:T(8,128)(2,1)} %q_hbm.1, bf16[16,1280]{1,0:T(8,128)(2,1)} %k_hbm.1, bf16[16,1280]{1,0:T(8,128)(2,1)} %v_hbm.1, bf16[16,1280]{1,0:T(8,128)(2,1)} %res_hbm.1, bf16[1280,1280]{1,0:T(8,128)(2,1)} %wo_hbm.1, f32[1,1280]{1,0:T(1,128)} %reshape.16.merge_gain_ref, ...), custom_call_target="tpu_custom_call" | custom-call | tf_op jit(solution)/shard_map/merge_step/pallas_call | solution.py:594
  79.4 1.5 %copy.16 = bf16[256,128]{1,0:T(8,128)(2,1)} copy(bf16[256,128]{1,0:T(8,128)(2,1)} %get-tuple-element.4) | data formatting | bytes 131072
  80.9 1.6 %copy.17 = f32[320,128]{1,0:T(8,128)} copy(f32[320,128]{1,0:T(8,128)} %get-tuple-element.5) | data formatting | bytes 327680

commit v2 on v1

--- a/solution.py
+++ b/solution.py
@@ -185,7 +185,8 @@
     mixed = res_buf[...].astype(F32) + dot(attended, wo_buf[...])
     inverse_rms = lax.rsqrt(jnp.sum(mixed * mixed, axis=1, keepdims=True) / DV + EPSILON)
     slot_valid = (iota((SLOTS, 1), 0).astype(F32) < own_valid).astype(F32)
-    own_buf[...] = (mixed * inverse_rms * merge_gain_ref[...] * slot_valid).astype(BF16)
+    merge_gain = jnp.concatenate([merge_gain_ref[i : i + 1, :] for i in range(10)], axis=1)
+    own_buf[...] = (mixed * inverse_rms * merge_gain * slot_valid).astype(BF16)
 
     def image_rows(zz, yy):
         return pl.ds(pl.multiple_of((zz * RING + yy) * SLOTS, SLOTS), SLOTS)
@@ -282,7 +283,7 @@
 
     add_chunk(0)
 
-    def first_axis(o, carry):
+    def first_axis(o):
         zz = (z + RING + shift(o)) % RING
         yy = (y + RING + shift(o)) % RING
         arrive(0, zz, y)
@@ -291,39 +292,15 @@
         arrive(1, z, yy)
         push(1, half_of(1, z, yy), z, yy, up_z)
         push(1, half_of(1, z, yy), z, yy, down_z)
-        add_chunk(o)
-        return carry
-
-    lax.fori_loop(1, RING, first_axis, 0)
-
-    sum_out[...] = sums[...].astype(BF16)
-
-    def routed(buf, peer):
-        return buf.at[pl.ds(pl.multiple_of(peer * BLOCK, BLOCK), BLOCK), :]
-
-    def exchange(out_buf, in_buf, send, recv):
-        def step(i, carry):
-            peer = (d + i) % GROUPS
-            remote(
-                routed(out_buf, peer), routed(in_buf, d), send, recv.at[d], {"dp": peer}
-            ).start()
-            return carry
-
-        lax.fori_loop(1, GROUPS, step, 0)
-        here = pl.ds(pl.multiple_of(d * BLOCK, BLOCK), BLOCK)
-        in_buf[here, :] = out_buf[here, :]
-
-    def exchanged(out_buf, in_buf, send, recv):
-        def step(i, carry):
-            peer = (d + i) % GROUPS
-            remote(
-                routed(out_buf, peer), routed(in_buf, peer), send, recv.at[peer], {"dp": peer}
-            ).wait_recv()
-            return carry
-
-        lax.fori_loop(1, GROUPS, step, 0)
-
-    exchange(sum_out, sum_in, sum_send, sum_recv)
+
+    def first_axis_pair(i, carry):
+        first_axis(2 * i + 1)
+        first_axis(2 * i + 2)
+        add_chunk(i + 1)
+        return carry
+
+    lax.fori_loop(0, 3, first_axis_pair, 0)
+    first_axis(7)
 
     def hop(h, o, up, down):
         zz = (z + RING + shift(o)) % RING
@@ -343,11 +320,48 @@
         if down:
             push(1, half_of(1, above, yy), above, yy, down_z)
 
-    def near_hops(i, carry):
-        hop(i // RING + 1, i % RING, True, True)
-        return carry
-
-    lax.fori_loop(0, 2 * RING, near_hops, 0)
+    def first_hop(i, carry):
+        hop(1, 2 * i, True, True)
+        hop(1, 2 * i + 1, True, True)
+        add_chunk(i + 4)
+        return carry
+
+    lax.fori_loop(0, RING // 2, first_hop, 0)
+
+    sum_out[...] = sums[...].astype(BF16)
+
+    def routed(buf, peer):
+        return buf.at[pl.ds(pl.multiple_of(peer * BLOCK, BLOCK), BLOCK), :]
+
+    def exchange(out_buf, in_buf, send, recv):
+        def step(i, carry):
+            peer = (d + i) % GROUPS
+            remote(
+                routed(out_buf, peer), routed(in_buf, d), send, recv.at[d], {"dp": peer}
+            ).start()
+            return carry
+
+        lax.fori_loop(1, GROUPS, step, 0)
+        here = pl.ds(pl.multiple_of(d * BLOCK, BLOCK), BLOCK)
+        in_buf[here, :] = out_buf[here, :]
+
+    def exchanged(out_buf, in_buf, send, recv):
+        def step(i, carry):
+            peer = (d + i) % GROUPS
+            remote(
+                routed(out_buf, peer), routed(in_buf, peer), send, recv.at[peer], {"dp": peer}
+            ).wait_recv()
+            return carry
+
+        lax.fori_loop(1, GROUPS, step, 0)
+
+    exchange(sum_out, sum_in, sum_send, sum_recv)
+
+    def second_hop(o, carry):
+        hop(2, o, True, True)
+        return carry
+
+    lax.fori_loop(0, RING, second_hop, 0)
 
     def third_hop(i, carry):
         hop(3, 2 * i, True, False)
@@ -372,20 +386,16 @@
         load.wait()
 
     def last_hop(o, carry):
-        arrive(0, (z + RING + shift(o)) % RING, (y + 4) % RING)
+        zz = (z + RING + shift(o)) % RING
+        arrive(0, zz, (y + 4) % RING)
         arrive(1, (z + 4) % RING, (y + RING + shift(o)) % RING)
-        return carry
-
-    lax.fori_loop(0, RING, last_hop, 0)
-
-    def project(b, carry):
-        here = pl.ds(pl.multiple_of(b * 128, 128), 128)
+        here = pl.ds(pl.multiple_of(zz * 128, 128), 128)
         product = dot(rows[here, :], w_buf[...])
         for j in range(4):
             wide[j, here, :] = product[:, j * COLS : (j + 1) * COLS]
         return carry
 
-    lax.fori_loop(0, ROWS // 128, project, 0)
+    lax.fori_loop(0, RING, last_hop, 0)
     outputs = wide[0, pl.ds(0, TOKENS, stride=4), :]
     for j in range(1, 4):
         outputs += wide[j, pl.ds(j, TOKENS, stride=4), :]
@@ -403,7 +413,6 @@
             squares[:, 128:256],
             inner[:, 0:128],
             inner[:, 128:256],
-            jnp.zeros((4, 128), F32),
         ],
         axis=0,
     )
@@ -466,49 +475,24 @@
     lax.fori_loop(0, ROWS // 128, narrow, 0)
 
     partner = {"dp": 2 * x + 1 - core}
-
-    def for_partner(i, carry):
-        first = pl.multiple_of((1 - core + 2 * i) * PIECE, 64)
-        here = pl.ds(pl.multiple_of(i * PIECE, 64), PIECE)
-        pair_out[here, :] = dot(rows_t[pl.ds(first, PIECE), :], spread[...]).astype(BF16)
-        remote(
-            pair_out.at[here, :],
-            pair_in.at[here, :],
-            pair_send.at[i],
-            pair_recv.at[i],
-            partner,
-        ).start()
-        return carry
-
-    lax.fori_loop(0, 2, for_partner, 0)
-
-    def for_self(i, carry):
-        first = pl.multiple_of((core + 2 * i) * PIECE, 64)
-        here = pl.ds(pl.multiple_of(i * PIECE, 64), PIECE)
-        kept[here, :] = dot(rows_t[pl.ds(first, PIECE), :], spread[...])
-        return carry
-
-    lax.fori_loop(0, 2, for_self, 0)
-
-    def pair_arrived(i, carry):
-        here = pl.ds(pl.multiple_of(i * PIECE, 64), PIECE)
-        remote(
-            pair_out.at[here, :], pair_in.at[here, :], pair_send.at[i], pair_recv.at[i], partner
-        ).wait_recv()
-        kept[here, :] = kept[here, :] + pair_in[here, :].astype(F32)
-        return carry
-
-    lax.fori_loop(0, 2, pair_arrived, 0)
-
+    offsets = ((4, 0), (3, 5), (2, 6), (1, 7))
     part = PIECE // 2
     ways = ((0, 1), (1, -1))
 
+    def group_dot(group, owner):
+        near, far = ((x + offset) % RING for offset in offsets[group])
+        first = pl.multiple_of((near % 2) * (2 * PIECE) + owner * PIECE, 64)
+        left = spread[:, pl.ds(pl.multiple_of((near // 2) * COLS, COLS), COLS)]
+        right = spread[:, pl.ds(pl.multiple_of((far // 2) * COLS, COLS), COLS)]
+        return dot(rows_t[pl.ds(first, PIECE), :], jnp.concatenate([left, right], axis=1))
+
+    def pair(group):
+        return remote(
+            pair_out.at[group], pair_in.at[group], pair_send.at[group], pair_recv.at[group], partner
+        )
+
     def reach(way, half):
         return 4 if way == half else 3
-
-    def kept_block(chip, half):
-        first = pl.multiple_of((chip % 2) * PIECE + half * part, 32)
-        return kept[pl.ds(first, part), pl.ds(pl.multiple_of((chip // 2) * COLS, COLS), COLS)]
 
     def chain(way, sign, half, step):
         return remote(
@@ -519,28 +503,53 @@
             {"dp": 2 * ((x + RING + sign) % RING) + core},
         )
 
-    for step in range(4):
-        for half in range(2):
+    places = {offset: (g, i) for g, two in enumerate(offsets) for i, offset in enumerate(two)}
+
+    def kept_block(offset, half):
+        group, side = places[offset % RING]
+        return kept[group, half * part : (half + 1) * part, side * COLS : (side + 1) * COLS]
+
+    def link(way, sign, half, step):
+        far = reach(way, half)
+        value = kept_block(sign * (far - step), half)
+        if step:
+            chain(way, sign, half, step - 1).wait_recv()
+            value = value + chain_in[way, half, step - 1].astype(F32)
+        chain_out[way, half, step] = value.astype(BF16)
+        chain(way, sign, half, step).start()
+
+    def finish_group(group):
+        pair(group).wait_recv()
+        kept[group] = kept[group] + pair_in[group].astype(F32)
+
+    for group in range(4):
+        pair_out[group] = group_dot(group, 1 - core).astype(BF16)
+        pair(group).start()
+        kept[group] = group_dot(group, core)
+    finish_group(0)
+    for way, sign in ways:
+        link(way, sign, way, 0)
+    finish_group(1)
+    for way, sign in ways:
+        link(way, sign, 1 - way, 0)
+    finish_group(2)
+    finish_group(3)
+    norm_out[...] = dot_first(pick[...], normed).astype(BF16)
+    exchange(norm_out, norm_in, norm_send, norm_recv)
+    for step in range(1, 4):
+        for way, sign in ways:
+            link(way, sign, way, step)
+        if step < 3:
             for way, sign in ways:
-                far = reach(way, half)
-                if step >= far:
-                    continue
-                value = kept_block((x + RING + sign * (far - step)) % RING, half)
-                if step:
-                    chain(way, sign, half, step - 1).wait_recv()
-                    value = value + chain_in[way, half, step - 1].astype(F32)
-                chain_out[way, half, step] = value.astype(BF16)
-                chain(way, sign, half, step).start()
-        if step == 0:
-            norm_out[...] = dot_first(pick[...], normed).astype(BF16)
-            exchange(norm_out, norm_in, norm_send, norm_recv)
-
-    exchanged(norm_out, norm_in, norm_send, norm_recv)
-    home = (pos_key[...] == iota((ROUTED, TOKENS), 1).astype(F32)).astype(F32).astype(BF16)
-    normed_out[...] = dot_first(home, norm_in[...]).astype(BF16)
+                link(way, sign, 1 - way, step)
+        if step == 2:
+            exchanged(norm_out, norm_in, norm_send, norm_recv)
+            home = pos_key[...] == iota((ROUTED, TOKENS), 1).astype(F32)
+            home = home.astype(F32).astype(BF16)
+            normed_out[...] = dot_first(home, norm_in[...]).astype(BF16)
 
     for half in range(2):
-        value = kept_block(x, half)
+        value = kept_block(0, half)
         for way, sign in ways:
             last = reach(way, half) - 1
             chain(way, sign, half, last).wait_recv()
@@ -562,11 +571,8 @@
         remote(
             in_buf.at[sent], in_buf.at[sent], stat_send.at[slot], recv.at[0], {"mp": (z + 1) % RING}
         ).wait_send()
-    for i in range(2):
-        here = pl.ds(i * PIECE, PIECE)
-        remote(
-            pair_out.at[here, :], pair_in.at[here, :], pair_send.at[i], pair_recv.at[i], partner
-        ).wait_send()
+    for group in range(4):
+        pair(group).wait_send()
     for half in range(2):
         for way, sign in ways:
             for step in range(reach(way, half)):
@@ -620,14 +626,14 @@
             pltpu.VMEM((ROUTED, COLS), BF16),
             pltpu.VMEM((TOKENS, ROUTED), BF16),
             pltpu.VMEM((TOKENS, COLS), F32),
-            pltpu.VMEM((2, 8, 128), F32),
-            pltpu.VMEM((RING, 8, 128), F32),
-            pltpu.VMEM((RING, 8, 128), F32),
+            pltpu.VMEM((2, 4, 128), F32),
+            pltpu.VMEM((RING, 4, 128), F32),
+            pltpu.VMEM((RING, 4, 128), F32),
             pltpu.VMEM((ROUTED, COLS), BF16),
             pltpu.VMEM((ROUTED, COLS), BF16),
-            pltpu.VMEM((2 * PIECE, 4 * COLS), F32),
-            pltpu.VMEM((2 * PIECE, 4 * COLS), BF16),
-            pltpu.VMEM((2 * PIECE, 4 * COLS), BF16),
+            pltpu.VMEM((4, PIECE, 2 * COLS), F32),
+            pltpu.VMEM((4, PIECE, 2 * COLS), BF16),
+            pltpu.VMEM((4, PIECE, 2 * COLS), BF16),
             pltpu.VMEM((2, 2, 4, part, COLS), BF16),
             pltpu.VMEM((2, 2, 4, part, COLS), BF16),
             dma((10,)),
@@ -640,8 +646,8 @@
             dma((RING,)),
             dma,
             dma((GROUPS,)),
-            dma((2,)),
-            dma((2,)),
+            dma((4,)),
+            dma((4,)),
             dma((2, 2, 4)),
             dma((2, 2, 4)),
         ],
@@ -653,7 +659,7 @@
         value_rows,
         residual,
         out_proj,
-        merge_gain.reshape(1, DV),
+        merge_gain.reshape(10, 128),
         merger_proj,
         model_gain.reshape(1, COLS),
         image_grid.T,

time: 83.5 us -> 79 us (0.946)
  Pallas kernels: 77.5 us -> 74.6 us
  local copies, waits for them, and re-layouts: 4.36 us -> 3.07 us
    pallas_call x1, Pallas kernels: 77.5 us -> 74.6 us  [on_device(): pl.pallas_call(kernel, out_shape=(jax.ShapeDtypeStruct((TOKENS, COLS), BF...]
    reshape x1 -> x0, local copies, waits for them, and re-layouts: 1.29 us -> none  [on_device(): merge_gain.reshape(1, DV)]
where the time goes in v2:
time: 79 us; the launch traced here: 78.4 us
  Pallas kernels  74.6 us (94%)
  local copies, waits for them, and re-layouts  3.07 us (4%)
    pallas_call x1, Pallas kernels, on_device(): pl.pallas_call(kernel, out_shape=(jax.ShapeDtypeStruct((TOKENS, COLS), BF...  74.6 us
    unnamed x2, local copies, waits for them, and re-layouts  3.07 us

profile of v2, /device:TPU:1, one launch (start us, length us, event | category | flops | bytes accessed | tf_op | source)
XLA Modules:
  0.0 78.4 jit_solution(1083562919511527457)
XLA Ops:
  0.6 74.6 %merge_step.1 = (bf16[256,128]{1,0:T(8,128)(2,1)}, f32[320,128]{1,0:T(8,128)}) custom-call(bf16[16,1280]{1,0:T(8,128)(2,1)} %q_hbm.1, bf16[16,1280]{1,0:T(8,128)(2,1)} %k_hbm.1, bf16[16,1280]{1,0:T(8,128)(2,1)} %v_hbm.1, bf16[16,1280]{1,0:T(8,128)(2,1)} %res_hbm.1, bf16[1280,1280]{1,0:T(8,128)(2,1)} %wo_hbm.1, f32[10,128]{1,0:T(8,128)} %bitcast.5, ...), custom_call_target="tpu_custom_call" | custom-call | tf_op jit(solution)/shard_map/merge_step/pallas_call | solution.py:600
  75.3 1.5 %copy.16 = bf16[256,128]{1,0:T(8,128)(2,1)} copy(bf16[256,128]{1,0:T(8,128)(2,1)} %get-tuple-element.4) | data formatting | bytes 131072
  76.8 1.6 %copy.17 = f32[320,128]{1,0:T(8,128)} copy(f32[320,128]{1,0:T(8,128)} %get-tuple-element.5) | data formatting | bytes 327680

commit v3 on v2

--- a/solution.py
+++ b/solution.py
@@ -92,8 +92,8 @@
     norm_out,
     norm_in,
     kept,
-    pair_out,
-    pair_in,
+    rows_p,
+    grad_pair,
     chain_out,
     chain_in,
     load_sem,
@@ -106,6 +106,8 @@
     y_recv,
     norm_send,
     norm_recv,
+    turn_send,
+    turn_recv,
     pair_send,
     pair_recv,
     chain_send,
@@ -236,6 +238,24 @@
     lax.fori_loop(1, RING, spread_own, 0)
     rows[image_rows(z, y), :] = own_buf[...]
 
+    partner = {"dp": 2 * x + 1 - core}
+
+    def finish_plane(plane):
+        here = pl.ds(pl.multiple_of(plane * 128, 128), 128)
+        product = dot(rows[here, :], w_buf[...])
+        for j in range(4):
+            wide[j, here, :] = product[:, j * COLS : (j + 1) * COLS]
+        rows_t[:, here] = rows[here, :].T
+        for t in range(2):
+            first = pl.multiple_of(2 * PIECE * t + (1 - core) * PIECE, 64)
+            remote(
+                rows_t.at[pl.ds(first, PIECE), here],
+                rows_p.at[pl.ds(t * PIECE, PIECE), here],
+                turn_send,
+                turn_recv,
+                partner,
+            ).start()
+
     groups = group_ref[...]
     arriving = groups == d
     arrived = arriving.astype(F32).astype(BF16)
@@ -389,10 +409,7 @@
         zz = (z + RING + shift(o)) % RING
         arrive(0, zz, (y + 4) % RING)
         arrive(1, (z + 4) % RING, (y + RING + shift(o)) % RING)
-        here = pl.ds(pl.multiple_of(zz * 128, 128), 128)
-        product = dot(rows[here, :], w_buf[...])
-        for j in range(4):
-            wide[j, here, :] = product[:, j * COLS : (j + 1) * COLS]
+        finish_plane(zz)
         return carry
 
     lax.fori_loop(0, RING, last_hop, 0)
@@ -442,17 +459,10 @@
         lax.fori_loop(1, RING, step, 0)
         return jnp.sum(in_buf[...], axis=0)
 
-    def turn(b, carry):
-        here = pl.ds(pl.multiple_of(b * 128, 128), 128)
-        rows_t[:, here] = rows[here, :].T
-        return carry
-
     share(0, "mp", z, z_in, z_recv)
-    lax.fori_loop(0, 4, turn, 0)
+    wide[...] = jnp.zeros_like(wide)
     packet[1] = shared(0, "mp", z, z_in, z_recv)
     share(1, "rep", y, y_in, y_recv)
-    lax.fori_loop(4, 8, turn, 0)
-    wide[...] = jnp.zeros_like(wide)
     totals = shared(1, "rep", y, y_in, y_recv)
 
     inverse_row = lax.rsqrt(totals[0:2, :] / D + EPSILON)
@@ -461,100 +471,102 @@
     inverse = jnp.concatenate([turned[:, 0:1], turned[:, 1:2]], axis=0)
     scale = jnp.concatenate([turned[:, 2:3], turned[:, 3:4]], axis=0)
     hidden = hidden_buf[...]
-    token_grad = (inverse * gain * sums[0:TOKENS, :] - hidden * scale).astype(BF16).astype(F32)
-    for j in range(4):
-        wide[j, pl.ds(j, TOKENS, stride=4), :] = token_grad
+    token_grad = (inverse * gain * sums[0:TOKENS, :] - hidden * scale).astype(BF16)
+    grad_pair[0] = token_grad
+    grad_copy = remote(grad_pair.at[0], grad_pair.at[1], pair_send, pair_recv, partner)
+    grad_copy.start()
     normed = (hidden * inverse * gain).astype(BF16)
 
-    def narrow(b, carry):
-        here = pl.ds(pl.multiple_of(b * 128, 128), 128)
+    def spread_rows(grads, side):
         for j in range(4):
-            spread[here, j * COLS : (j + 1) * COLS] = wide[j, here, :].astype(BF16)
-        return carry
-
-    lax.fori_loop(0, ROWS // 128, narrow, 0)
-
-    partner = {"dp": 2 * x + 1 - core}
+            wide[j, pl.ds(j, TOKENS, stride=4), :] = grads
+
+        def narrow(b, carry):
+            here = pl.ds(pl.multiple_of(b * 128, 128), 128)
+            for j in range(4):
+                spread[side, here, j * COLS : (j + 1) * COLS] = wide[j, here, :].astype(BF16)
+            return carry
+
+        lax.fori_loop(0, ROWS // 128, narrow, 0)
+
     offsets = ((4, 0), (3, 5), (2, 6), (1, 7))
-    part = PIECE // 2
+    part = PIECE // 4
     ways = ((0, 1), (1, -1))
 
-    def group_dot(group, owner):
+    def group_dot(group, side):
         near, far = ((x + offset) % RING for offset in offsets[group])
-        first = pl.multiple_of((near % 2) * (2 * PIECE) + owner * PIECE, 64)
-        left = spread[:, pl.ds(pl.multiple_of((near // 2) * COLS, COLS), COLS)]
-        right = spread[:, pl.ds(pl.multiple_of((far // 2) * COLS, COLS), COLS)]
-        return dot(rows_t[pl.ds(first, PIECE), :], jnp.concatenate([left, right], axis=1))
-
-    def pair(group):
-        return remote(
-            pair_out.at[group], pair_in.at[group], pair_send.at[group], pair_recv.at[group], partner
-        )
+        left = spread[side, :, pl.ds(pl.multiple_of((near // 2) * COLS, COLS), COLS)]
+        right = spread[side, :, pl.ds(pl.multiple_of((far // 2) * COLS, COLS), COLS)]
+        both = jnp.concatenate([left, right], axis=1)
+        if side == 0:
+            first = pl.multiple_of((near % 2) * (2 * PIECE) + core * PIECE, 64)
+            return dot(rows_t[pl.ds(first, PIECE), :], both)
+        return dot(rows_p[pl.ds(pl.multiple_of((near % 2) * PIECE, 64), PIECE), :], both)
 
     def reach(way, half):
         return 4 if way == half else 3
 
-    def chain(way, sign, half, step):
+    def chain(way, sign, half, chunk, step):
         return remote(
-            chain_out.at[way, half, step],
-            chain_in.at[way, half, step],
-            chain_send.at[way, half, step],
-            chain_recv.at[way, half, step],
+            chain_out.at[way, half, chunk, step],
+            chain_in.at[way, half, chunk, step],
+            chain_send.at[way, half, chunk, step],
+            chain_recv.at[way, half, chunk, step],
             {"dp": 2 * ((x + RING + sign) % RING) + core},
         )
 
     places = {offset: (g, i) for g, two in enumerate(offsets) for i, offset in enumerate(two)}
 
-    def kept_block(offset, half):
+    def kept_block(offset, half, chunk):
         group, side = places[offset % RING]
-        return kept[group, half * part : (half + 1) * part, side * COLS : (side + 1) * COLS]
-
-    def link(way, sign, half, step):
-        far = reach(way, half)
-        value = kept_block(sign * (far - step), half)
-        if step:
-            chain(way, sign, half, step - 1).wait_recv()
-            value = value + chain_in[way, half, step - 1].astype(F32)
-        chain_out[way, half, step] = value.astype(BF16)
-        chain(way, sign, half, step).start()
-
-    def finish_group(group):
-        pair(group).wait_recv()
-        kept[group] = kept[group] + pair_in[group].astype(F32)
-
+        first = (2 * half + chunk) * part
+        return kept[group, first : first + part, side * COLS : (side + 1) * COLS]
+
+    def link(long, step):
+        for chunk in range(2):
+            for way, sign in ways:
+                half = way if long else 1 - way
+                far = reach(way, half)
+                value = kept_block(sign * (far - step), half, chunk)
+                if step:
+                    chain(way, sign, half, chunk, step - 1).wait_recv()
+                    value = value + chain_in[way, half, chunk, step - 1].astype(F32)
+                chain_out[way, half, chunk, step] = value.astype(BF16)
+                chain(way, sign, half, chunk, step).start()
+
+    spread_rows(token_grad.astype(F32), 0)
     for group in range(4):
-        pair_out[group] = group_dot(group, 1 - core).astype(BF16)
-        pair(group).start()
-        kept[group] = group_dot(group, core)
-    finish_group(0)
-    for way, sign in ways:
-        link(way, sign, way, 0)
-    finish_group(1)
-    for way, sign in ways:
-        link(way, sign, 1 - way, 0)
-    finish_group(2)
-    finish_group(3)
+        kept[group] = group_dot(group, 0)
+    grad_copy.wait_recv()
+    spread_rows(grad_pair[1].astype(F32), 1)
+    remote(rows_p, rows_p, turn_send, turn_recv, partner).wait_recv()
+    for group in range(4):
+        kept[group] = kept[group] + group_dot(group, 1)
+        if group == 0:
+            link(True, 0)
+        if group == 1:
+            link(False, 0)
     norm_out[...] = dot_first(pick[...], normed).astype(BF16)
     exchange(norm_out, norm_in, norm_send, norm_recv)
     for step in range(1, 4):
-        for way, sign in ways:
-            link(way, sign, way, step)
+        link(True, step)
         if step < 3:
-            for way, sign in ways:
-                link(way, sign, 1 - way, step)
+            link(False, step)
         if step == 2:
             exchanged(norm_out, norm_in, norm_send, norm_recv)
             home = pos_key[...] == iota((ROUTED, TOKENS), 1).astype(F32)
             home = home.astype(F32).astype(BF16)
             normed_out[...] = dot_first(home, norm_in[...]).astype(BF16)
 
-    for half in range(2):
-        value = kept_block(0, half)
-        for way, sign in ways:
-            last = reach(way, half) - 1
-            chain(way, sign, half, last).wait_recv()
-            value = value + chain_in[way, half, last].astype(F32)
-        grad_out[half * part : (half + 1) * part, :] = value
+    for half in (1, 0):
+        for chunk in range(2):
+            value = kept_block(0, half, chunk)
+            for way, sign in ways[:: -1 if half else 1]:
+                last = reach(way, half) - 1
+                chain(way, sign, half, chunk, last).wait_recv()
+                value = value + chain_in[way, half, chunk, last].astype(F32)
+            first = (2 * half + chunk) * part
+            grad_out[first : first + part, :] = value
 
     for half in range(2):
         sent = rows.at[pl.ds(0, (MEMBERS - 1) * SLOTS), pl.ds(half * HALF, HALF)]
@@ -571,12 +583,13 @@
         remote(
             in_buf.at[sent], in_buf.at[sent], stat_send.at[slot], recv.at[0], {"mp": (z + 1) % RING}
         ).wait_send()
-    for group in range(4):
-        pair(group).wait_send()
+    grad_copy.wait_send()
+    remote(rows_p, rows_p, turn_send, turn_recv, partner).wait_send()
     for half in range(2):
-        for way, sign in ways:
-            for step in range(reach(way, half)):
-                chain(way, sign, half, step).wait_send()
+        for chunk in range(2):
+            for way, sign in ways:
+                for step in range(reach(way, half)):
+                    chain(way, sign, half, chunk, step).wait_send()
 
 
 def on_device(
@@ -596,7 +609,7 @@
     hbm = pl.BlockSpec(memory_space=pl.ANY)
     vmem = pl.BlockSpec(memory_space=pltpu.VMEM)
     dma = pltpu.SemaphoreType.DMA
-    part = PIECE // 2
+    part = PIECE // 4
     return pl.pallas_call(
         kernel,
         out_shape=(
@@ -617,7 +630,7 @@
             pltpu.VMEM((ROWS, DV), BF16),
             pltpu.VMEM((DV, ROWS), BF16),
             pltpu.VMEM((4, ROWS, COLS), F32),
-            pltpu.VMEM((ROWS, 4 * COLS), BF16),
+            pltpu.VMEM((2, ROWS, 4 * COLS), BF16),
             pltpu.VMEM((ROUTED, 1), F32),
             pltpu.VMEM((ROUTED, 1), F32),
             pltpu.VMEM((8, 512), F32),
@@ -632,10 +645,10 @@
             pltpu.VMEM((ROUTED, COLS), BF16),
             pltpu.VMEM((ROUTED, COLS), BF16),
             pltpu.VMEM((4, PIECE, 2 * COLS), F32),
-            pltpu.VMEM((4, PIECE, 2 * COLS), BF16),
-            pltpu.VMEM((4, PIECE, 2 * COLS), BF16),
-            pltpu.VMEM((2, 2, 4, part, COLS), BF16),
-            pltpu.VMEM((2, 2, 4, part, COLS), BF16),
+            pltpu.VMEM((2 * PIECE, ROWS), BF16),
+            pltpu.VMEM((2, TOKENS, COLS), BF16),
+            pltpu.VMEM((2, 2, 2, 4, part, COLS), BF16),
+            pltpu.VMEM((2, 2, 2, 4, part, COLS), BF16),
             dma((10,)),
             dma((2,)),
             dma((2, MEMBERS)),
@@ -646,10 +659,12 @@
             dma((RING,)),
             dma,
             dma((GROUPS,)),
-            dma((4,)),
-            dma((4,)),
-            dma((2, 2, 4)),
-            dma((2, 2, 4)),
+            dma,
+            dma,
+            dma,
+            dma,
+            dma((2, 2, 2, 4)),
+            dma((2, 2, 2, 4)),
         ],
         compiler_params=pltpu.CompilerParams(collective_id=0, has_side_effects=True),
         name="merge_step",

time: 79 us -> 78.8 us (level)
  no operation moved by 1% of the time
where the time goes in v3:
time: 78.8 us; the launch traced here: 78.3 us
  Pallas kernels  74.6 us (95%)
  local copies, waits for them, and re-layouts  3.07 us (4%)
    pallas_call x1, Pallas kernels, on_device(): pl.pallas_call(kernel, out_shape=(jax.ShapeDtypeStruct((TOKENS, COLS), BF...  74.6 us
    unnamed x2, local copies, waits for them, and re-layouts  3.07 us

profile of v3, /device:TPU:1, one launch (start us, length us, event | category | flops | bytes accessed | tf_op | source)
XLA Modules:
  0.0 78.3 jit_solution(15498031350797197893)
XLA Ops:
  0.6 74.6 %merge_step.1 = (bf16[256,128]{1,0:T(8,128)(2,1)}, f32[320,128]{1,0:T(8,128)}) custom-call(bf16[16,1280]{1,0:T(8,128)(2,1)} %q_hbm.1, bf16[16,1280]{1,0:T(8,128)(2,1)} %k_hbm.1, bf16[16,1280]{1,0:T(8,128)(2,1)} %v_hbm.1, bf16[16,1280]{1,0:T(8,128)(2,1)} %res_hbm.1, bf16[1280,1280]{1,0:T(8,128)(2,1)} %wo_hbm.1, f32[10,128]{1,0:T(8,128)} %bitcast.5, ...), custom_call_target="tpu_custom_call" | custom-call | tf_op jit(solution)/shard_map/merge_step/pallas_call | solution.py:613
  75.2 1.5 %copy.16 = bf16[256,128]{1,0:T(8,128)(2,1)} copy(bf16[256,128]{1,0:T(8,128)(2,1)} %get-tuple-element.4) | data formatting | bytes 131072
  76.7 1.6 %copy.17 = f32[320,128]{1,0:T(8,128)} copy(f32[320,128]{1,0:T(8,128)} %get-tuple-element.5) | data formatting | bytes 327680

commit v4 on v3

--- a/solution.py
+++ b/solution.py
@@ -57,15 +57,20 @@
     v_hbm,
     res_hbm,
     wo_hbm,
+    merge_gain_hbm,
+    w_hbm,
+    gain_hbm,
+    grid_hbm,
+    group_hbm,
+    roll_hbm,
+    cot_hbm,
+    normed_out,
+    grad_out,
     merge_gain_ref,
-    w_hbm,
     gain_ref,
     grid_ref,
     group_ref,
     roll_ref,
-    cot_hbm,
-    normed_out,
-    grad_out,
     q_buf,
     k_buf,
     v_buf,
@@ -119,6 +124,13 @@
     x = d // 2
     core = d % 2
 
+    smalls = [
+        pltpu.make_async_copy(grid_hbm, grid_ref, load_sem.at[10]),
+        pltpu.make_async_copy(merge_gain_hbm, merge_gain_ref, load_sem.at[11]),
+        pltpu.make_async_copy(group_hbm, group_ref, load_sem.at[12]),
+        pltpu.make_async_copy(roll_hbm, roll_ref, load_sem.at[13]),
+        pltpu.make_async_copy(gain_hbm, gain_ref, load_sem.at[14]),
+    ]
     loads = [
         pltpu.make_async_copy(q_hbm, q_buf, load_sem.at[0]),
         pltpu.make_async_copy(k_hbm, k_buf, load_sem.at[1]),
@@ -132,7 +144,8 @@
         )
         for j in range(4)
     ]
-    for load in loads:
+    smalls[0].start()
+    for load in loads[:5] + smalls[1:] + loads[5:]:
         load.start()
 
     barrier = pltpu.get_barrier_semaphore()
@@ -150,6 +163,7 @@
     greet("rep", y, RING)
     greet("dp", d, GROUPS)
 
+    smalls[0].wait()
     factors = grid_ref[...]
     products = factors[0:1, :] * factors[1:2, :]
     counts = jnp.concatenate(
@@ -187,6 +201,7 @@
     mixed = res_buf[...].astype(F32) + dot(attended, wo_buf[...])
     inverse_rms = lax.rsqrt(jnp.sum(mixed * mixed, axis=1, keepdims=True) / DV + EPSILON)
     slot_valid = (iota((SLOTS, 1), 0).astype(F32) < own_valid).astype(F32)
+    smalls[1].wait()
     merge_gain = jnp.concatenate([merge_gain_ref[i : i + 1, :] for i in range(10)], axis=1)
     own_buf[...] = (mixed * inverse_rms * merge_gain * slot_valid).astype(BF16)
 
@@ -240,22 +255,27 @@
 
     partner = {"dp": 2 * x + 1 - core}
 
-    def finish_plane(plane):
+    def project(plane):
         here = pl.ds(pl.multiple_of(plane * 128, 128), 128)
         product = dot(rows[here, :], w_buf[...])
         for j in range(4):
             wide[j, here, :] = product[:, j * COLS : (j + 1) * COLS]
-        rows_t[:, here] = rows[here, :].T
-        for t in range(2):
-            first = pl.multiple_of(2 * PIECE * t + (1 - core) * PIECE, 64)
-            remote(
-                rows_t.at[pl.ds(first, PIECE), here],
-                rows_p.at[pl.ds(t * PIECE, PIECE), here],
-                turn_send,
-                turn_recv,
-                partner,
-            ).start()
-
+
+    def turn(half, plane):
+        here = pl.ds(pl.multiple_of(plane * 128, 128), 128)
+        features = slice(half * HALF, (half + 1) * HALF)
+        rows_t[features, here] = rows[here, features].T
+        first = pl.multiple_of(HALF * half + (1 - core) * PIECE, 64)
+        remote(
+            rows_t.at[pl.ds(first, PIECE), here],
+            rows_p.at[pl.ds(half * PIECE, PIECE), here],
+            turn_send,
+            turn_recv,
+            partner,
+        ).start()
+
+    for load in smalls[2:]:
+        load.wait()
     groups = group_ref[...]
     arriving = groups == d
     arrived = arriving.astype(F32).astype(BF16)
@@ -346,7 +366,10 @@
         add_chunk(i + 4)
         return carry
 
+    turn(1, z)
     lax.fori_loop(0, RING // 2, first_hop, 0)
+    turn(1, (z + 1) % RING)
+    turn(1, (z + 7) % RING)
 
     sum_out[...] = sums[...].astype(BF16)
 
@@ -382,6 +405,8 @@
         return carry
 
     lax.fori_loop(0, RING, second_hop, 0)
+    turn(1, (z + 2) % RING)
+    turn(1, (z + 6) % RING)
 
     def third_hop(i, carry):
         hop(3, 2 * i, True, False)
@@ -389,6 +414,8 @@
         return carry
 
     lax.fori_loop(0, RING // 2, third_hop, 0)
+    turn(1, (z + 3) % RING)
+    turn(1, (z + 5) % RING)
 
     own_half = (d % 2) * MEMBERS
     own_dest = jnp.sum(
@@ -409,10 +436,12 @@
         zz = (z + RING + shift(o)) % RING
         arrive(0, zz, (y + 4) % RING)
         arrive(1, (z + 4) % RING, (y + RING + shift(o)) % RING)
-        finish_plane(zz)
+        turn(0, zz)
+        project(zz)
         return carry
 
     lax.fori_loop(0, RING, last_hop, 0)
+    turn(1, (z + 4) % RING)
     outputs = wide[0, pl.ds(0, TOKENS, stride=4), :]
     for j in range(1, 4):
         outputs += wide[j, pl.ds(j, TOKENS, stride=4), :]
@@ -534,6 +563,8 @@
                 chain_out[way, half, chunk, step] = value.astype(BF16)
                 chain(way, sign, half, chunk, step).start()
 
+    norm_out[...] = dot_first(pick[...], normed).astype(BF16)
+    exchange(norm_out, norm_in, norm_send, norm_recv)
     spread_rows(token_grad.astype(F32), 0)
     for group in range(4):
         kept[group] = group_dot(group, 0)
@@ -546,8 +577,6 @@
             link(True, 0)
         if group == 1:
             link(False, 0)
-    norm_out[...] = dot_first(pick[...], normed).astype(BF16)
-    exchange(norm_out, norm_in, norm_send, norm_recv)
     for step in range(1, 4):
         link(True, step)
         if step < 3:
@@ -606,7 +635,7 @@
     rollout_image,
     cotangent,
 ):
-    hbm = pl.BlockSpec(memory_space=pl.ANY)
+    hbm = pl.BlockSpec(memory_space=pltpu.HBM)
     vmem = pl.BlockSpec(memory_space=pltpu.VMEM)
     dma = pltpu.SemaphoreType.DMA
     part = PIECE // 4
@@ -616,9 +645,14 @@
             jax.ShapeDtypeStruct((TOKENS, COLS), BF16),
             jax.ShapeDtypeStruct((PIECE, COLS), F32),
         ),
-        in_specs=[hbm, hbm, hbm, hbm, hbm, vmem, hbm, vmem, vmem, vmem, vmem, hbm],
+        in_specs=[hbm] * 12,
         out_specs=(vmem, vmem),
         scratch_shapes=[
+            pltpu.VMEM((10, 128), F32),
+            pltpu.VMEM((1, COLS), F32),
+            pltpu.VMEM((2, GROUPS * MEMBERS), jnp.int32),
+            pltpu.VMEM((8, 128), jnp.int32),
+            pltpu.VMEM((8, 128), jnp.int32),
             pltpu.VMEM((SLOTS, DV), BF16),
             pltpu.VMEM((SLOTS, DV), BF16),
             pltpu.VMEM((SLOTS, DV), BF16),
@@ -649,7 +683,7 @@
             pltpu.VMEM((2, TOKENS, COLS), BF16),
             pltpu.VMEM((2, 2, 2, 4, part, COLS), BF16),
             pltpu.VMEM((2, 2, 2, 4, part, COLS), BF16),
-            dma((10,)),
+            dma((15,)),
             dma((2,)),
             dma((2, MEMBERS)),
             dma,
@@ -666,9 +700,9 @@
             dma((2, 2, 2, 4)),
             dma((2, 2, 2, 4)),
         ],
-        compiler_params=pltpu.CompilerParams(collective_id=0, has_side_effects=True),
+        compiler_params=pltpu.CompilerParams(collective_id=0, has_side_effects=True, vmem_limit_bytes=36 << 20),
         name="merge_step",
-    )(
+    )(*(pltpu.with_memory_space_constraint(value, pltpu.HBM) for value in (
         query_rows,
         key_rows,
         value_rows,
@@ -681,7 +715,7 @@
         image_group.reshape(8, 128),
         rollout_image.reshape(8, 128),
         cotangent,
-    )
+    )))
 
 
 def solution(mesh):

time: 78.8 us -> 75.4 us (0.957); the launches traced: 78.3 us -> 73.9 us
  Pallas kernels: 74.6 us -> 72 us
  local copies, waits for them, and re-layouts: 3.07 us -> 1.3 us
    pallas_call x1, Pallas kernels: 74.6 us -> 72 us  [on_device(): pl.pallas_call(kernel, out_shape=(jax.ShapeDtypeStruct((TOKENS, COLS), BF...]
    unnamed x2, local copies, waits for them, and re-layouts: 3.07 us -> 1.3 us
where the time goes in v4:
time: 75.4 us; the launch traced here: 73.9 us
  Pallas kernels  72 us (95%)
  local copies, waits for them, and re-layouts  1.3 us (2%)
    pallas_call x1, Pallas kernels, on_device(): pl.pallas_call(kernel, out_shape=(jax.ShapeDtypeStruct((TOKENS, COLS), BF...  72 us

profile of v4, /device:TPU:1, one launch (start us, length us, event | category | flops | bytes accessed | tf_op | source)
XLA Modules:
  0.0 73.9 jit_solution(6983064942656933465)
XLA Ops:
  0.6 72.0 %merge_step.1 = (bf16[256,128]{1,0:T(8,128)(2,1)S(1)}, f32[320,128]{1,0:T(8,128)S(1)}) custom-call(bf16[16,1280]{1,0:T(8,128)(2,1)} %q_hbm.1, bf16[16,1280]{1,0:T(8,128)(2,1)} %k_hbm.1, bf16[16,1280]{1,0:T(8,128)(2,1)} %v_hbm.1, bf16[16,1280]{1,0:T(8,128)(2,1)} %res_hbm.1, bf16[1280,1280]{1,0:T(8,128)(2,1)} %wo_hbm.1, f32[10,128]{1,0:T(8,128)} %bitcast.5, ...), custom_call_target="tpu_custom_call" | custom-call | tf_op jit(solution)/shard_map/merge_step/pallas_call | solution.py:642
  72.6 0.6 copy.16
  73.2 0.7 copy.17

commit v5 on v4

--- a/solution.py
+++ b/solution.py
@@ -124,6 +124,21 @@
     x = d // 2
     core = d % 2
 
+    barrier = pltpu.get_barrier_semaphore()
+
+    def greet(axis, me, size):
+        def step(i, carry):
+            pl.semaphore_signal(
+                barrier, inc=1, device_id={axis: (me + i) % size}, device_id_type=MESH
+            )
+            return carry
+
+        lax.fori_loop(1, size, step, 0)
+
+    greet("mp", z, RING)
+    greet("rep", y, RING)
+    greet("dp", d, GROUPS)
+
     smalls = [
         pltpu.make_async_copy(grid_hbm, grid_ref, load_sem.at[10]),
         pltpu.make_async_copy(merge_gain_hbm, merge_gain_ref, load_sem.at[11]),
@@ -147,21 +162,6 @@
     smalls[0].start()
     for load in loads[:5] + smalls[1:] + loads[5:]:
         load.start()
-
-    barrier = pltpu.get_barrier_semaphore()
-
-    def greet(axis, me, size):
-        def step(i, carry):
-            pl.semaphore_signal(
-                barrier, inc=1, device_id={axis: (me + i) % size}, device_id_type=MESH
-            )
-            return carry
-
-        lax.fori_loop(1, size, step, 0)
-
-    greet("mp", z, RING)
-    greet("rep", y, RING)
-    greet("dp", d, GROUPS)
 
     smalls[0].wait()
     factors = grid_ref[...]
@@ -321,7 +321,6 @@
         part = cot_buf[pl.ds(pl.multiple_of(a * 512, 512), 512), :]
         sums[...] += dot(chosen, part)
 
-    add_chunk(0)
 
     def first_axis(o):
         zz = (z + RING + shift(o)) % RING
@@ -333,14 +332,11 @@
         push(1, half_of(1, z, yy), z, yy, up_z)
         push(1, half_of(1, z, yy), z, yy, down_z)
 
-    def first_axis_pair(i, carry):
-        first_axis(2 * i + 1)
-        first_axis(2 * i + 2)
-        add_chunk(i + 1)
+    def first_axis_step(o, carry):
+        first_axis(o)
         return carry
 
-    lax.fori_loop(0, 3, first_axis_pair, 0)
-    first_axis(7)
+    lax.fori_loop(1, RING, first_axis_step, 0)
 
     def hop(h, o, up, down):
         zz = (z + RING + shift(o)) % RING
@@ -363,7 +359,7 @@
     def first_hop(i, carry):
         hop(1, 2 * i, True, True)
         hop(1, 2 * i + 1, True, True)
-        add_chunk(i + 4)
+        add_chunk(i)
         return carry
 
     turn(1, z)
@@ -371,6 +367,13 @@
     turn(1, (z + 1) % RING)
     turn(1, (z + 7) % RING)
 
+    def second_hop(i, carry):
+        hop(2, 2 * i, True, True)
+        hop(2, 2 * i + 1, True, True)
+        add_chunk(i + 4)
+        return carry
+
+    lax.fori_loop(0, RING // 2, second_hop, 0)
     sum_out[...] = sums[...].astype(BF16)
 
     def routed(buf, peer):
@@ -400,11 +403,6 @@
 
     exchange(sum_out, sum_in, sum_send, sum_recv)
 
-    def second_hop(o, carry):
-        hop(2, o, True, True)
-        return carry
-
-    lax.fori_loop(0, RING, second_hop, 0)
     turn(1, (z + 2) % RING)
     turn(1, (z + 6) % RING)
 
@@ -436,12 +434,10 @@
         zz = (z + RING + shift(o)) % RING
         arrive(0, zz, (y + 4) % RING)
         arrive(1, (z + 4) % RING, (y + RING + shift(o)) % RING)
-        turn(0, zz)
         project(zz)
         return carry
 
     lax.fori_loop(0, RING, last_hop, 0)
-    turn(1, (z + 4) % RING)
     outputs = wide[0, pl.ds(0, TOKENS, stride=4), :]
     for j in range(1, 4):
         outputs += wide[j, pl.ds(j, TOKENS, stride=4), :]
@@ -488,10 +484,16 @@
         lax.fori_loop(1, RING, step, 0)
         return jnp.sum(in_buf[...], axis=0)
 
+    def turn_first(plane, carry):
+        turn(0, plane)
+        return carry
+
     share(0, "mp", z, z_in, z_recv)
-    wide[...] = jnp.zeros_like(wide)
+    lax.fori_loop(0, RING, turn_first, 0)
+    turn(1, (z + 4) % RING)
     packet[1] = shared(0, "mp", z, z_in, z_recv)
     share(1, "rep", y, y_in, y_recv)
+    wide[...] = jnp.zeros_like(wide)
     totals = shared(1, "rep", y, y_in, y_recv)
 
     inverse_row = lax.rsqrt(totals[0:2, :] / D + EPSILON)
@@ -503,7 +505,15 @@
     token_grad = (inverse * gain * sums[0:TOKENS, :] - hidden * scale).astype(BF16)
     grad_pair[0] = token_grad
     grad_copy = remote(grad_pair.at[0], grad_pair.at[1], pair_send, pair_recv, partner)
-    grad_copy.start()
+
+    def send_grad(i, carry):
+        here = pl.ds(pl.multiple_of(i * 32, 32), 32)
+        remote(
+            grad_pair.at[0, here], grad_pair.at[1, here], pair_send, pair_recv, partner
+        ).start()
+        return carry
+
+    lax.fori_loop(0, TOKENS // 32, send_grad, 0)
     normed = (hidden * inverse * gain).astype(BF16)
 
     def spread_rows(grads, side):
@@ -581,7 +591,7 @@
         link(True, step)
         if step < 3:
             link(False, step)
-        if step == 2:
+        if step == 3:
             exchanged(norm_out, norm_in, norm_send, norm_recv)
             home = pos_key[...] == iota((ROUTED, TOKENS), 1).astype(F32)
             home = home.astype(F32).astype(BF16)

time: 75.4 us -> 75.4 us (level)
  the two profiles are of different devices: /device:TPU:1 before, /device:TPU:4 now
where the time goes in v5:
time: 75.4 us; the launch traced here: 75.2 us
  Pallas kernels  73.3 us (97%)
  local copies, waits for them, and re-layouts  1.3 us (2%)
    pallas_call x1, Pallas kernels, on_device(): pl.pallas_call(kernel, out_shape=(jax.ShapeDtypeStruct((TOKENS, COLS), BF...  73.3 us

profile of v5, /device:TPU:4, one launch (start us, length us, event | category | flops | bytes accessed | tf_op | source)
XLA Modules:
  0.0 75.2 jit_solution(15718957453426733676)
XLA Ops:
  0.6 73.3 %merge_step.1 = (bf16[256,128]{1,0:T(8,128)(2,1)S(1)}, f32[320,128]{1,0:T(8,128)S(1)}) custom-call(bf16[16,1280]{1,0:T(8,128)(2,1)} %q_hbm.1, bf16[16,1280]{1,0:T(8,128)(2,1)} %k_hbm.1, bf16[16,1280]{1,0:T(8,128)(2,1)} %v_hbm.1, bf16[16,1280]{1,0:T(8,128)(2,1)} %res_hbm.1, bf16[1280,1280]{1,0:T(8,128)(2,1)} %wo_hbm.1, f32[10,128]{1,0:T(8,128)} %bitcast.5, ...), custom_call_target="tpu_custom_call" | custom-call | tf_op jit(solution)/shard_map/merge_step/pallas_call | solution.py:652
  73.9 0.6 copy.16
  74.6 0.7 copy.17
